TPU v7x, 32 devices: a whole 2x2x4 slice. The times are simulated.
32 devices in a mesh: dp: 8 (over z, x), tensor: 4 (over y, core).
Axes of the slice: x: 2, y: 2, z: 4, core: 2. Of those that a mesh axis runs over, the one named last changes fastest.
Arguments:
- tokens: bfloat16 [16384, 768], P(('dp', 'tensor')), may hold values from -6 to 6
- segments: int32 [16, 1024], P('dp'), may hold values from 0 to 23, never falling along the last dimension, each value on 1 to 512 neighbouring positions
- query_weight: float32 [768, 768], P('dp', 'tensor'), may hold values from -0.21875 to 0.21875
- query_bias: float32 [768], P('tensor'), may hold values from -1.5 to 1.5
- key_weight: float32 [768, 768], P('dp', 'tensor'), may hold values from -0.21875 to 0.21875
- value_weight: float32 [768, 768], P('dp', 'tensor'), may hold values from -0.21875 to 0.21875
- value_bias: float32 [768], P('tensor'), may hold values from -1.5 to 1.5
- out_weight: float32 [768, 768], P('dp', 'tensor'), may hold values from -1 to 1
- out_bias: float32 [768], replicated, may hold values from -1.5 to 1.5
- attn_gain: float32 [768], replicated, may hold values from 0.5 to 1.5
- attn_shift: float32 [768], replicated, may hold values from -1.5 to 1.5
- inner_weight: float32 [768, 3072], P('dp', 'tensor'), may hold values from -0.21875 to 0.21875
- inner_bias: float32 [3072], P('tensor'), may hold values from -1.5 to 1.5
- outer_weight: float32 [768, 3072], P('dp', 'tensor'), may hold values from -0.109375 to 0.109375
- outer_bias: float32 [768], replicated, may hold values from -1.5 to 1.5
- ffn_gain: float32 [768], replicated, may hold values from 0.5 to 1.5
- ffn_shift: float32 [768], replicated, may hold values from -1.5 to 1.5
- out_grad: bfloat16 [16384, 768], P(('dp', 'tensor')), may hold values from -6 to 6
Outputs:
- layer_out: bfloat16 [16384, 768], P(('dp', 'tensor'))
- tokens_grad: float32 [16384, 768], P(('dp', 'tensor'))
- query_weight_grad: float32 [768, 768], P('dp', 'tensor')
- query_bias_grad: float32 [768], P('tensor')
- key_weight_grad: float32 [768, 768], P('dp', 'tensor')
- value_weight_grad: float32 [768, 768], P('dp', 'tensor')
- value_bias_grad: float32 [768], P('tensor')
- out_weight_grad: float32 [768, 768], P('dp', 'tensor')
- out_bias_grad: float32 [768], replicated
- attn_gain_grad: float32 [768], replicated
- attn_shift_grad: float32 [768], replicated
- inner_weight_grad: float32 [768, 3072], P('dp', 'tensor')
- inner_bias_grad: float32 [3072], P('tensor')
- outer_weight_grad: float32 [768, 3072], P('dp', 'tensor')
- outer_bias_grad: float32 [768], replicated
- ffn_gain_grad: float32 [768], replicated
- ffn_shift_grad: float32 [768], replicated
Inputs may be any that keep to these rules, and one draw needn't show every extreme that they name: `segments`: within each sequence the document ids never fall; a document spans 1 to 512 tokens, and some document spans exactly 512.
All inputs are finite; a program needn't handle non-finite values.
Results may differ from a plain program's by a relative error of at most 0.014.
The roundings to bfloat16 on the way count: a program that leaves them out, or rounds other values in their place, can miss the bound.
Values may be sent and summed in bfloat16 or wider, within the bound.
No kernel may reach another device: no remote copies, remote signals or barrier semaphores. Data moves between devices by JAX's collectives and lax.ppermute only.
A program may use at most 128 MiB of HBM per device.

v0:
```python
import math

import jax
import jax.numpy as jnp
from jax import lax
from jax.sharding import PartitionSpec as P

HD = 64


NEG_FILL = -1e30
ROOT_HALF = 0.7071067811865476
INV_ROOT_TAU = 0.3989422804014327


def normalize_rows(residual, norm_gain, norm_shift):
    center = residual - jnp.mean(residual, axis=-1, keepdims=True)
    inv_spread = lax.rsqrt(jnp.mean(center * center, axis=-1, keepdims=True) + 1e-06)
    normed = center * inv_spread
    return (normed * norm_gain + norm_shift, normed, inv_spread)


def normalize_back(upstream, normed, inv_spread, norm_gain):
    scaled = upstream * norm_gain
    inner_term = (
        scaled
        - jnp.mean(scaled, axis=-1, keepdims=True)
        - normed * jnp.mean(scaled * normed, axis=-1, keepdims=True)
    )
    return (inv_spread * inner_term, jnp.sum(upstream * normed, axis=0), jnp.sum(upstream, axis=0))


def gelu_slope(pre_act):
    return (
        0.5 * (1.0 + lax.erf(pre_act * ROOT_HALF))
        + pre_act * jnp.exp(-0.5 * pre_act * pre_act) * INV_ROOT_TAU
    )


def masked_scores(queries, key_rows, seg_rows, seg_cols, scale):
    scores = (
        jnp.einsum("qhd,khd->hqk", queries, key_rows, preferred_element_type=jnp.float32) * scale
    )
    same_doc = seg_rows[:, None] == seg_cols[None, :]
    return jnp.where(same_doc[None, :, :], scores, NEG_FILL)


def shards(
    tokens,
    segments,
    query_weight,
    query_bias,
    key_weight,
    value_weight,
    value_bias,
    out_weight,
    out_bias,
    attn_gain,
    attn_shift,
    inner_weight,
    inner_bias,
    outer_weight,
    outer_bias,
    ffn_gain,
    ffn_shift,
    out_grad,
):
    share_rows = tokens.shape[0]
    model_width = tokens.shape[1]
    seq_count = segments.shape[0]
    seq_len = segments.shape[1]
    head_width = query_bias.shape[0]
    heads_here = head_width // HD
    unit_count = inner_bias.shape[0]
    group_rows = seq_count * seq_len
    tensor_rank = lax.axis_index("tensor")
    row_start = tensor_rank * share_rows
    scale = 1.0 / math.sqrt(HD)
    block_len = min(512, seq_len)

    def own_rows(full_rows):
        return lax.dynamic_slice_in_dim(full_rows, row_start, share_rows, 0)

    def heads_view(flat_rows):
        return flat_rows.reshape(seq_count, seq_len, heads_here, HD)

    all_tokens = lax.all_gather(tokens, "tensor", axis=0, tiled=True)
    query_mat, key_mat, value_mat, out_mat, inner_mat, outer_mat = (
        lax.all_gather(query_weight.astype(jnp.bfloat16), "dp", axis=0, tiled=True),
        lax.all_gather(key_weight.astype(jnp.bfloat16), "dp", axis=0, tiled=True),
        lax.all_gather(value_weight.astype(jnp.bfloat16), "dp", axis=0, tiled=True),
        lax.all_gather(out_weight.astype(jnp.bfloat16), "dp", axis=0, tiled=True),
        lax.all_gather(inner_weight.astype(jnp.bfloat16), "dp", axis=0, tiled=True),
        lax.all_gather(outer_weight.astype(jnp.bfloat16), "dp", axis=0, tiled=True),
    )
    query_low = (
        jnp.dot(all_tokens, query_mat, preferred_element_type=jnp.float32) + query_bias
    ).astype(jnp.bfloat16)
    key_low = jnp.dot(all_tokens, key_mat, preferred_element_type=jnp.float32).astype(jnp.bfloat16)
    value_low = (
        jnp.dot(all_tokens, value_mat, preferred_element_type=jnp.float32) + value_bias
    ).astype(jnp.bfloat16)

    def attend_forward(scan_item):
        queries, key_rows, value_rows, segment = scan_item
        mixed_parts = []
        lse_parts = []
        for offset in range(0, seq_len, block_len):
            scores = masked_scores(
                queries[offset : offset + block_len],
                key_rows,
                segment[offset : offset + block_len],
                segment,
                scale,
            )
            row_max = jnp.max(scores, axis=-1, keepdims=True)
            exp_scores = jnp.exp(scores - row_max)
            row_total = jnp.sum(exp_scores, axis=-1, keepdims=True)
            prob_low = (exp_scores / row_total).astype(jnp.bfloat16)
            mixed_block = jnp.einsum(
                "hqk,khd->qhd", prob_low, value_rows, preferred_element_type=jnp.float32
            )
            mixed_parts.append(mixed_block.astype(jnp.bfloat16))
            lse_parts.append(row_max + jnp.log(row_total))
        return (jnp.concatenate(mixed_parts, axis=0), jnp.concatenate(lse_parts, axis=1))

    mixed_heads, log_totals = lax.map(
        attend_forward,
        (heads_view(query_low), heads_view(key_low), heads_view(value_low), segments),
    )
    mixed_flat = mixed_heads.reshape(group_rows, head_width)
    attn_part = jnp.einsum("rh,dh->rd", mixed_flat, out_mat, preferred_element_type=jnp.float32)
    attn_total = lax.psum(attn_part, "tensor")
    hidden_full, normed_full, inv_full = normalize_rows(
        all_tokens.astype(jnp.float32) + attn_total + out_bias, attn_gain, attn_shift
    )
    hidden_low = hidden_full.astype(jnp.bfloat16)
    normed_one = own_rows(normed_full)
    inv_one = own_rows(inv_full)
    inner_pre = jnp.dot(hidden_low, inner_mat, preferred_element_type=jnp.float32) + inner_bias
    active_low = jax.nn.gelu(inner_pre, approximate=False).astype(jnp.bfloat16)
    ffn_part = jnp.einsum("rf,df->rd", active_low, outer_mat, preferred_element_type=jnp.float32)
    ffn_total = lax.psum(ffn_part, "tensor")
    out_full, normed_full_two, inv_full_two = normalize_rows(
        hidden_full + ffn_total + outer_bias, ffn_gain, ffn_shift
    )
    layer_out = own_rows(out_full).astype(jnp.bfloat16)
    normed_two = own_rows(normed_full_two)
    inv_two = own_rows(inv_full_two)
    grad_two, ffn_gain_part, ffn_shift_part = normalize_back(
        out_grad.astype(jnp.float32), normed_two, inv_two, ffn_gain
    )
    grad_two_low = lax.all_gather(grad_two.astype(jnp.bfloat16), "tensor", axis=0, tiled=True)
    outer_w_grad = jnp.einsum(
        "rd,rf->df", grad_two_low, active_low, preferred_element_type=jnp.float32
    )
    inner_grad = jnp.dot(grad_two_low, outer_mat, preferred_element_type=jnp.float32) * gelu_slope(
        inner_pre
    )
    inner_bias_part = jnp.sum(inner_grad, axis=0)
    inner_low = inner_grad.astype(jnp.bfloat16)
    inner_w_grad = jnp.einsum(
        "rd,rf->df", hidden_low, inner_low, preferred_element_type=jnp.float32
    )
    back_part = jnp.einsum("rf,df->rd", inner_low, inner_mat, preferred_element_type=jnp.float32)
    back_share = lax.psum_scatter(back_part, "tensor", scatter_dimension=0, tiled=True)
    grad_one, attn_gain_part, attn_shift_part = normalize_back(
        grad_two + back_share, normed_one, inv_one, attn_gain
    )
    grad_one_low = lax.all_gather(grad_one.astype(jnp.bfloat16), "tensor", axis=0, tiled=True)
    out_w_grad = jnp.einsum(
        "rd,rh->dh", grad_one_low, mixed_flat, preferred_element_type=jnp.float32
    )
    mixed_grad = jnp.dot(grad_one_low, out_mat, preferred_element_type=jnp.float32).astype(
        jnp.bfloat16
    )

    def attend_back(scan_item):
        queries, key_rows, value_rows, segment, log_rows, grad_rows = scan_item
        query_parts = []
        key_acc = jnp.zeros(key_rows.shape, jnp.float32)
        value_acc = jnp.zeros(value_rows.shape, jnp.float32)
        for offset in range(0, seq_len, block_len):
            query_block = queries[offset : offset + block_len]
            grad_block = grad_rows[offset : offset + block_len]
            scores = masked_scores(
                query_block, key_rows, segment[offset : offset + block_len], segment, scale
            )
            probs = jnp.exp(scores - log_rows[:, offset : offset + block_len])
            prob_low = probs.astype(jnp.bfloat16)
            value_acc = value_acc + jnp.einsum(
                "hqk,qhd->khd", prob_low, grad_block, preferred_element_type=jnp.float32
            )
            prob_grad = jnp.einsum(
                "qhd,khd->hqk", grad_block, value_rows, preferred_element_type=jnp.float32
            )
            row_dot = jnp.sum(probs * prob_grad, axis=-1, keepdims=True)
            score_low = (probs * (prob_grad - row_dot)).astype(jnp.bfloat16)
            query_parts.append(
                jnp.einsum("hqk,khd->qhd", score_low, key_rows, preferred_element_type=jnp.float32)
                * scale
            )
            key_acc = (
                key_acc
                + jnp.einsum(
                    "hqk,qhd->khd", score_low, query_block, preferred_element_type=jnp.float32
                )
                * scale
            )
        return (jnp.concatenate(query_parts, axis=0), key_acc, value_acc)

    query_grad, key_grad, value_grad = lax.map(
        attend_back,
        (
            heads_view(query_low),
            heads_view(key_low),
            heads_view(value_low),
            segments,
            log_totals,
            heads_view(mixed_grad),
        ),
    )
    query_grad = query_grad.reshape(group_rows, head_width)
    key_grad = key_grad.reshape(group_rows, head_width)
    value_grad = value_grad.reshape(group_rows, head_width)
    query_bias_part = jnp.sum(query_grad, axis=0)
    value_bias_part = jnp.sum(value_grad, axis=0)
    query_grad_low = query_grad.astype(jnp.bfloat16)
    key_grad_low = key_grad.astype(jnp.bfloat16)
    value_grad_low = value_grad.astype(jnp.bfloat16)
    query_w_grad = jnp.einsum(
        "rd,rh->dh", all_tokens, query_grad_low, preferred_element_type=jnp.float32
    )
    key_w_grad = jnp.einsum(
        "rd,rh->dh", all_tokens, key_grad_low, preferred_element_type=jnp.float32
    )
    value_w_grad = jnp.einsum(
        "rd,rh->dh", all_tokens, value_grad_low, preferred_element_type=jnp.float32
    )
    input_part = (
        jnp.einsum("rh,dh->rd", query_grad_low, query_mat, preferred_element_type=jnp.float32)
        + jnp.einsum("rh,dh->rd", key_grad_low, key_mat, preferred_element_type=jnp.float32)
        + jnp.einsum("rh,dh->rd", value_grad_low, value_mat, preferred_element_type=jnp.float32)
    )
    input_share = lax.psum_scatter(
        input_part.astype(jnp.bfloat16), "tensor", scatter_dimension=0, tiled=True
    ).astype(jnp.float32)
    tokens_grad = grad_one + input_share
    query_wsum, key_wsum, value_wsum, out_wsum, inner_wsum, outer_wsum = (
        lax.psum_scatter(query_w_grad, "dp", scatter_dimension=0, tiled=True),
        lax.psum_scatter(key_w_grad, "dp", scatter_dimension=0, tiled=True),
        lax.psum_scatter(value_w_grad, "dp", scatter_dimension=0, tiled=True),
        lax.psum_scatter(out_w_grad, "dp", scatter_dimension=0, tiled=True),
        lax.psum_scatter(inner_w_grad, "dp", scatter_dimension=0, tiled=True),
        lax.psum_scatter(outer_w_grad, "dp", scatter_dimension=0, tiled=True),
    )

    def padded(local_part, full_len):
        return lax.dynamic_update_slice_in_dim(
            jnp.zeros((full_len,), jnp.float32), local_part, tensor_rank * local_part.shape[0], 0
        )

    (
        query_bsum,
        value_bsum,
        out_bsum,
        attn_gsum,
        attn_ssum,
        inner_bsum,
        outer_bsum,
        ffn_gsum,
        ffn_ssum,
    ) = lax.psum(
        (
            padded(query_bias_part, model_width),
            padded(value_bias_part, model_width),
            jnp.sum(grad_one, axis=0),
            attn_gain_part,
            attn_shift_part,
            padded(inner_bias_part, unit_count * lax.axis_size("tensor")),
            jnp.sum(grad_two, axis=0),
            ffn_gain_part,
            ffn_shift_part,
        ),
        ("dp", "tensor"),
    )
    query_bias_grad = lax.dynamic_slice_in_dim(query_bsum, tensor_rank * head_width, head_width, 0)
    value_bias_grad = lax.dynamic_slice_in_dim(value_bsum, tensor_rank * head_width, head_width, 0)
    inner_bias_grad = lax.dynamic_slice_in_dim(inner_bsum, tensor_rank * unit_count, unit_count, 0)
    return (
        layer_out,
        tokens_grad,
        query_wsum,
        query_bias_grad,
        key_wsum,
        value_wsum,
        value_bias_grad,
        out_wsum,
        out_bsum,
        attn_gsum,
        attn_ssum,
        inner_wsum,
        inner_bias_grad,
        outer_wsum,
        outer_bsum,
        ffn_gsum,
        ffn_ssum,
    )


def solution(mesh):
    in_specs = (
        P(("dp", "tensor"), None),
        P("dp", None),
        P("dp", "tensor"),
        P("tensor"),
        P("dp", "tensor"),
        P("dp", "tensor"),
        P("tensor"),
        P("dp", "tensor"),
        P(),
        P(),
        P(),
        P("dp", "tensor"),
        P("tensor"),
        P("dp", "tensor"),
        P(),
        P(),
        P(),
        P(("dp", "tensor"), None),
    )
    out_specs = (
        P(("dp", "tensor"), None),
        P(("dp", "tensor"), None),
        P("dp", "tensor"),
        P("tensor"),
        P("dp", "tensor"),
        P("dp", "tensor"),
        P("tensor"),
        P("dp", "tensor"),
        P(),
        P(),
        P(),
        P("dp", "tensor"),
        P("tensor"),
        P("dp", "tensor"),
        P(),
        P(),
        P(),
    )
    return jax.shard_map(shards, mesh=mesh, in_specs=in_specs, out_specs=out_specs, check_vma=False)
```

profile of v0, /device:TPU:0, one launch (start us, length us, event | category | flops | bytes accessed | tf_op | source)
XLA Modules:
  0.0 1161.3 jit_solution(236222957657964434)
XLA Ops:
  12.4 33.1 %all_gather.31 = bf16[768,192]{1,0:T(8,128)(2,1)S(1)} all-gather(bf16[96,192]{1,0:T(8,128)(2,1)S(1)} %convert_element_type.115), channel_id=1, replica_groups=mesh['dp'=8,'tensor'=4] {'dp'}, dimensions={0}, use_global_device_ids=true | all-gather | bytes 331776 | tf_op jit(solution)/shard_map/all_gather | solution.py:92
  45.5 33.1 %all_gather.28 = bf16[768,192]{1,0:T(8,128)(2,1)} all-gather(bf16[96,192]{1,0:T(8,128)(2,1)S(1)} %convert_element_type.109), channel_id=1, replica_groups=mesh['dp'=8,'tensor'=4] {'dp'}, dimensions={0}, use_global_device_ids=true | all-gather | bytes 331776 | tf_op jit(solution)/shard_map/all_gather | solution.py:91
  78.7 31.2 %all_gather.30 = bf16[768,192]{1,0:T(8,128)(2,1)S(1)} all-gather(bf16[96,192]{1,0:T(8,128)(2,1)S(1)} %convert_element_type.113), channel_id=1, replica_groups=mesh['dp'=8,'tensor'=4] {'dp'}, dimensions={0}, use_global_device_ids=true | all-gather | bytes 331776 | tf_op jit(solution)/shard_map/all_gather | solution.py:90
  109.9 30.9 %all_gather.29 = bf16[768,192]{1,0:T(8,128)(2,1)S(1)} all-gather(bf16[96,192]{1,0:T(8,128)(2,1)S(1)} %convert_element_type.111), channel_id=1, replica_groups=mesh['dp'=8,'tensor'=4] {'dp'}, dimensions={0}, use_global_device_ids=true | all-gather | bytes 331776 | tf_op jit(solution)/shard_map/all_gather | solution.py:89
  140.9 3.2 fusion.101
  144.9 3.1 convolution_convert_fusion.1
  148.8 3.1 fusion.100
  152.7 26.5 %while.26 = (s32[]{:T(128)}, bf16[2,1024,3,64]{1,3,2,0:T(8,128)(2,1)}, f32[2,3,1024,1]{2,1,3,0:T(4,128)}, bf16[2,1024,3,64]{1,3,2,0:T(8,128)(2,1)S(1)}, s32[2,10...) while((s32[]{:T(128)}, ...), condition=%wide.region_5.6_spmd, body=%wide.region_0.5_spmd.sunk | while | flops 845086720 | bytes 51743492 | solution.py:127
  156.5 3.5 fusion.200
  160.0 2.2 fusion.202
  162.2 2.2 fusion.201
  169.6 3.5 fusion.200
  173.1 2.2 fusion.202
  175.4 2.2 fusion.201
  179.2 1.9 copy.62
  182.2 3.7 fusion.124
  187.7 118.9 %all-reduce.4.cloned.1.call-done = f32[2048,768]{1,0:T(8,128)} async-done(((f32[2048,768]{1,0:T(8,128)}), f32[2048,768]{1,0:T(8,128)}) %all-reduce.4.cloned.1.call-update) | async-done | bytes 6291472 | tf_op jit(solution)/shard_map/psum | solution.py:133
  306.6 4.7 fusion.105
  313.1 1.8 multiply_reduce_fusion.3
  314.9 3.2 subtract_multiply_fusion.1
  318.2 18.8 %fusion.86 = (bf16[2048,768]{1,0:T(8,128)(2,1)}, f32[2048,768]{1,0:T(8,128)}) fusion(f32[768]{0:T(1024)S(1)} %copy-done.49, bf16[768,768]{1,0:T(8,128)(2,1)} %all-gather.8.cloned.1.call-done, f32[2048,768]{1,0:T(8,128)} %subtract_multiply_fusion.1, f32[768]{0:T(1024)S(1)} %copy-done.35, f32[768]{0:T(1024)S(1)} %copy-done.28), kind=kOutput, calls=%fused_computation.117 | convolution fusion | flops 2524446720 | bytes 16917504 | tf_op jit(solution)/shard_map/dot_general | solution.py:140
  337.0 7.5 fusion.125
  344.5 119.9 %all-reduce.6.cloned.1.call-done = f32[2048,768]{1,0:T(8,128)} async-done(((f32[2048,768]{1,0:T(8,128)}), f32[2048,768]{1,0:T(8,128)}) %all-reduce.6.cloned.1.call-update) | async-done | bytes 6291472 | tf_op jit(solution)/shard_map/psum | solution.py:143
  464.4 5.8 fusion.120
  473.3 2.0 fusion.117
  477.6 28.8 %all-gather.12.cloned.1.call-done = bf16[2048,768]{1,0:T(8,128)(2,1)} async-done(((bf16[512,768]{1,0:T(8,128)(2,1)}), bf16[2048,768]{1,0:T(8,128)(2,1)}) %all-gather.12.cloned.1.call-update) | async-done | bytes 3145744 | tf_op jit(solution)/shard_map/all_gather | solution.py:153
  506.4 8.4 fusion.123
  516.5 4.5 fusion.112
  521.1 58.4 %reduce-scatter.15.cloned.1.call-done = f32[512,768]{1,0:T(8,128)} async-done(((f32[2048,768]{1,0:T(8,128)}), f32[512,768]{1,0:T(8,128)}) %reduce-scatter.15.cloned.1.call-update) | async-done | bytes 1572880 | tf_op jit(solution)/shard_map/reduce_scatter | solution.py:166
  579.5 3.6 multiply_reduce_fusion.4
  583.1 2.4 fusion.119
  587.7 28.6 %all-gather.14.cloned.1.call-done = bf16[2048,768]{1,0:T(8,128)(2,1)} async-done(((bf16[512,768]{1,0:T(8,128)(2,1)}), bf16[2048,768]{1,0:T(8,128)(2,1)}) %all-gather.14.cloned.1.call-update) | async-done | bytes 3145744 | tf_op jit(solution)/shard_map/all_gather | solution.py:170
  616.4 4.0 convolution_convert_fusion
  620.3 2.6 reshape.319
  624.0 72.8 %while.27 = (s32[]{:T(128)}, f32[2,1024,3,64]{1,3,2,0:T(8,128)}, bf16[2,1024,3,64]{1,3,2,0:T(8,128)(2,1)}, f32[2,1024,3,64]{1,3,2,0:T(8,128)}, bf16[2,1024,3,64]...) while((s32[]{:T(128)}, f32[2,1024,3,64]{1,3,2,0:T(8,128)}, ...), condition=%wide.region_20.21_spmd, body=%wide.region_17.20_spmd.sunk | while | flops 2062480384 | bytes 156913616 | solution.py:212
  627.8 1.9 fusion.222
  629.7 2.8 fusion.223
  632.5 5.3 multiply_reduce_fusion.9
  637.8 5.3 multiply_reduce_fusion.10
  643.1 7.6 multiply_convert_fusion.3
  650.7 3.1 fusion.217
  664.0 1.9 fusion.222
  665.9 2.8 fusion.223
  668.7 5.3 multiply_reduce_fusion.9
  674.0 5.3 multiply_reduce_fusion.10
  679.3 7.6 multiply_convert_fusion.3
  686.9 3.1 fusion.217
  696.8 3.3 fusion.121
  705.4 2.8 add_convert_fusion
  708.3 6.9 fusion.129
  715.3 8.9 fusion.110
  724.6 4.0 fusion.128
  728.7 2.7 convolution_bitcast_fusion
  732.7 3.7 convolution_bitcast_fusion.2
  736.4 2.2 copy.73
  738.7 2.7 convolution_bitcast_fusion.1
  743.6 41.2 %all-reduce = (f32[768]{0:T(1024)S(1)}, f32[768]{0:T(1024)S(1)}, f32[768]{0:T(1024)}, f32[768]{0:T(1024)}, f32[768]{0:T(1024)}, /*index=5*/f32[3072]{0:T(1024)S(1)}, f32[768]{0:T(1024)}, f32[768]{0:T(1024)}, f32[768]{0:T(1024)}) all-reduce(f32[768]{0:T(1024)S(1)} %dynamic_update_slice.27, ...), channel_id=1, replica_groups=mesh['dp'=8,'tensor'=4] {'dp','tensor'}, use_global_device_ids=true, to_apply=%region_24.25 | all-reduce | flops 9216 | bytes 73728 | tf_op jit(solution)/shard_map/psum | solution.py:273
  786.7 2.4 convert_add_fusion
  789.1 30.7 %reduce-scatter.23.cloned.1.call-done = f32[96,768]{1,0:T(8,128)} async-done(((f32[768,768]{1,0:T(8,128)}), f32[96,768]{1,0:T(8,128)}) %reduce-scatter.23.cloned.1.call-update) | async-done | bytes 294928 | tf_op jit(solution)/shard_map/reduce_scatter | solution.py:255
  819.8 72.1 %reduce-scatter.21.cloned.1.call-done = f32[96,768]{1,0:T(8,128)} async-done(((f32[768,768]{1,0:T(8,128)}), f32[96,768]{1,0:T(8,128)}) %reduce-scatter.21.cloned.1.call-update) | async-done | bytes 294928 | tf_op jit(solution)/shard_map/reduce_scatter | solution.py:254
  891.9 65.2 %reduce-scatter.19.cloned.1.call-done = f32[96,192]{1,0:T(8,128)} async-done(((f32[768,192]{1,0:T(8,128)}), f32[96,192]{1,0:T(8,128)}) %reduce-scatter.19.cloned.1.call-update) | async-done | bytes 73744 | tf_op jit(solution)/shard_map/reduce_scatter | solution.py:253
  957.1 65.7 %reduce-scatter.29.cloned.1.call-done = f32[96,192]{1,0:T(8,128)} async-done(((f32[768,192]{1,0:T(8,128)}), f32[96,192]{1,0:T(8,128)}) %reduce-scatter.29.cloned.1.call-update) | async-done | bytes 73744
  1022.8 65.2 %reduce-scatter.25.cloned.1.call-done = f32[96,192]{1,0:T(8,128)} async-done(((f32[768,192]{1,0:T(8,128)}), f32[96,192]{1,0:T(8,128)}) %reduce-scatter.25.cloned.1.call-update) | async-done | bytes 73744
  1088.0 65.7 %reduce-scatter.27.cloned.1.call-done = f32[96,192]{1,0:T(8,128)} async-done(((f32[768,192]{1,0:T(8,128)}), f32[96,192]{1,0:T(8,128)}) %reduce-scatter.27.cloned.1.call-update) | async-done | bytes 73744
  (259 shorter events, 62.8 us)
Async XLA Ops:
  8.0 132.9 %all-gather.6.cloned.1.call-start = ((), (), s32[]{:S(2)}) async-start(), calls=%async_computation.8 | async-start | bytes 3932160 | tf_op jit(solution)/shard_map/all_gather | solution.py:87
  8.8 297.8 %all-reduce.4.cloned.1.call-start = ((), (), s32[]{:S(2)}) async-start(), calls=%async_computation.9 | async-start | bytes 12582912 | tf_op jit(solution)/shard_map/psum | solution.py:133
  109.9 38.0 %copy-start.13 = (bf16[768,192]{1,0:T(8,128)(2,1)}, bf16[768,192]{1,0:T(8,128)(2,1)S(1)}, u32[]{:S(2)}) copy-start(bf16[768,192]{1,0:T(8,128)(2,1)S(1)} %all_gather.30) | copy-start | bytes 884740
  140.9 7.1 copy-start.17
  144.1 4.7 copy-start.50
  148.0 4.7 copy-start.22
  162.2 2.3 copy-start.32
  162.2 2.3 copy-start.23
  175.4 2.3 copy-start.32
  175.4 2.3 copy-start.23
  182.2 3.8 copy-start.30
  186.0 120.6 %copy-start.37 = (f32[768]{0:T(1024)S(1)}, f32[768]{0:T(1024)}, u32[]{:S(2)}) copy-start(f32[768]{0:T(1024)} %param.30) | copy-start | bytes 9220
  186.0 132.2 %all-gather.8.cloned.1.call-start = ((), (), s32[]{:S(2)}) async-start(), calls=%async_computation.10 | async-start | bytes 1327104 | tf_op jit(solution)/shard_map/all_gather | solution.py:93
  186.7 150.2 %all-gather.10.cloned.1.call-start = ((), (), s32[]{:S(2)}) async-start(), calls=%async_computation.11 | async-start | bytes 1327104 | tf_op jit(solution)/shard_map/all_gather | solution.py:94
  187.6 276.8 %all-reduce.6.cloned.1.call-start = ((), (), s32[]{:S(2)}) async-start(), calls=%async_computation.12 | async-start | bytes 12582912 | tf_op jit(solution)/shard_map/psum | solution.py:143
  306.6 4.8 copy-start.1
  306.6 6.5 copy-start.4
  314.9 3.3 copy-start.28
  314.9 3.3 copy-start.35
  314.9 3.3 copy-start.49
  344.5 120.0 %copy-start.45 = (f32[768]{0:T(1024)S(1)}, f32[768]{0:T(1024)}, u32[]{:S(2)}) copy-start(f32[768]{0:T(1024)} %param.36) | copy-start | bytes 9220
  344.5 161.9 %all-gather.12.cloned.1.call-start = ((), (), s32[]{:S(2)}) async-start(), calls=%async_computation.13 | async-start | bytes 3932160 | tf_op jit(solution)/shard_map/all_gather | solution.py:153
  471.1 2.2 copy-start.46
  475.3 1.1 copy-start.9
  477.5 102.0 %reduce-scatter.15.cloned.1.call-start = ((), (), s32[]{:S(2)}) async-start(), calls=%async_computation.14 | async-start | bytes 7864320 | tf_op jit(solution)/shard_map/reduce_scatter | solution.py:166
  506.4 10.1 copy-start.48
  514.8 1.7 copy-start.16
  521.0 95.3 %all-gather.14.cloned.1.call-start = ((), (), s32[]{:S(2)}) async-start(), calls=%async_computation.15 | async-start | bytes 3932160 | tf_op jit(solution)/shard_map/all_gather | solution.py:170
  585.5 1.1 copy-start.7
  585.5 38.5 %copy-start.34 = (f32[2,3,1024,1]{2,1,3,0:T(4,128)S(1)}, f32[2,3,1024,1]{2,1,3,0:T(4,128)}, u32[]{:S(2)}) copy-start(f32[2,3,1024,1]{2,1,3,0:T(4,128)} %get-tuple-element.494) | copy-start | bytes 73732
  587.7 199.0 %reduce-scatter.17.cloned.1.call-start = ((), (), s32[]{:S(2)}) async-start(), calls=%async_computation.16 | async-start | bytes 3932160 | tf_op jit(solution)/shard_map/reduce_scatter | solution.py:245
  624.2 3.6 copy-start.2
  625.7 2.1 copy-start.10
  650.7 5.8 copy-start
  650.7 5.8 copy-start.25
  653.8 4.5 copy-start.19
  656.6 3.8 copy-start.3
  656.6 3.8 copy-start.6
  660.4 3.6 copy-start.2
  661.9 2.1 copy-start.10
  686.9 5.8 copy-start
  686.9 5.8 copy-start.25
  690.0 4.5 copy-start.19
  692.7 3.8 copy-start.3
  692.8 3.8 copy-start.6
  696.8 5.4 copy-start.27
  696.8 6.4 copy-start.14
  708.2 7.1 copy-start.29
  708.2 7.1 copy-start.36
  708.3 111.5 %reduce-scatter.23.cloned.1.call-start = ((), (), s32[]{:S(2)}) async-start(), calls=%async_computation.19 | async-start | bytes 2654208 | tf_op jit(solution)/shard_map/reduce_scatter | solution.py:255
  715.2 9.3 copy-start.12
  715.3 176.7 %reduce-scatter.21.cloned.1.call-start = ((), (), s32[]{:S(2)}) async-start(), calls=%async_computation.18 | async-start | bytes 2654208 | tf_op jit(solution)/shard_map/reduce_scatter | solution.py:254
  724.3 232.8 %reduce-scatter.19.cloned.1.call-start = ((), (), s32[]{:S(2)}) async-start(), calls=%async_computation.17 | async-start | bytes 884736 | tf_op jit(solution)/shard_map/reduce_scatter | solution.py:253
  728.7 294.1 %reduce-scatter.29.cloned.1.call-start = ((), (), s32[]{:S(2)}) async-start(), calls=%async_computation.22 | async-start | bytes 884736
  732.6 10.1 copy-start.47
  732.6 10.9 copy-start.39
  732.6 10.9 copy-start.40
  732.6 10.9 copy-start.41
  732.6 10.9 copy-start.42
  732.6 10.9 copy-start.43
  732.7 10.9 copy-start.44
  732.7 54.0 %copy-start.8 = (f32[512,768]{1,0:T(8,128)S(1)}, f32[512,768]{1,0:T(8,128)}, u32[]{:S(2)}) copy-start(f32[512,768]{1,0:T(8,128)} %copy-done.7) | copy-start | bytes 4718596
  732.7 355.3 %reduce-scatter.25.cloned.1.call-start = ((), (), s32[]{:S(2)}) async-start(), calls=%async_computation.20 | async-start | bytes 884736
  738.7 415.1 %reduce-scatter.27.cloned.1.call-start = ((), (), s32[]{:S(2)}) async-start(), calls=%async_computation.21 | async-start | bytes 884736
  (16 other events, 15.2 us)
Sparse Core Ops, SparseCore 0:
  10.4 31.2 all-gather.5
  186.1 120.4 all-reduce.3
  344.6 119.7 all-reduce.5
  477.6 28.7 all-gather.11
  521.1 58.3 reduce-scatter.14
  587.8 28.5 all-gather.13
  708.3 37.9 reduce-scatter.16
  750.4 69.3 reduce-scatter.22
  823.9 67.9 reduce-scatter.20
  895.6 61.4 reduce-scatter.18
  961.3 61.4 reduce-scatter.28
  1026.5 61.4 reduce-scatter.24
  1092.2 61.4 reduce-scatter.26
Sparse Core Ops, SparseCore 1:
  189.2 42.3 all-gather.7
  234.2 40.0 all-gather.9
where the time goes:
time: 1170 us; the launch traced here: 1160 us
  waiting for transfers between devices  720 us (62%)
  blocking collectives  170 us (15%)
  matrix products  154 us (13%)
  other arithmetic  64.1 us (5%)
  local copies, waits for them, and re-layouts  34.6 us (3%)
  between operations  16.5 us (1%)
    unnamed x18, waiting for transfers between devices  198 us
    psum x1, waiting for transfers between devices, shards(): ffn_total = lax.psum(ffn_part, 'tensor')  120 us
    psum x1, waiting for transfers between devices, shards(): attn_total = lax.psum(attn_part, 'tensor')  119 us
    reduce_scatter x1, waiting for transfers between devices, shards(): lax.psum_scatter(inner_w_grad, 'dp', scatter_dimension=0, tiled=True)  72.1 us
    reduce_scatter x1, waiting for transfers between devices, shards(): lax.psum_scatter(out_w_grad, 'dp', scatter_dimension=0, tiled=True)  65.2 us
    reduce_scatter x1, waiting for transfers between devices, shards(): lax.psum_scatter(back_part, 'tensor', scatter_dimension=0, tiled=True)  58.4 us
    psum x1, blocking collectives, shards(): lax.psum((padded(query_bias_part, model_width), padded(value_bias_part, m...  41.2 us
    all_gather x1, blocking collectives, shards(): lax.all_gather(value_weight.astype(jnp.bfloat16), 'dp', axis=0, tiled=True)  33.1 us
  transfers between devices with their start and end apart: 15, of which 11 were waited for; matrix products, arithmetic and copies ran while one was open for 6% of the time, Pallas kernels for 0%

commit v1 on v0

v1 whole, which is shorter than its diff:
```python
import math

import jax
import jax.numpy as jnp
from jax import lax
from jax.sharding import Mesh
from jax.sharding import PartitionSpec as P

HD = 64
NEG_FILL = -1e30
ROOT_HALF = 0.7071067811865476
INV_ROOT_TAU = 0.3989422804014327
bf16 = jnp.bfloat16
f32 = jnp.float32


def normalize_rows(residual, norm_gain, norm_shift):
    center = residual - jnp.mean(residual, axis=-1, keepdims=True)
    inv_spread = lax.rsqrt(jnp.mean(center * center, axis=-1, keepdims=True) + 1e-06)
    normed = center * inv_spread
    return (normed * norm_gain + norm_shift, normed, inv_spread)


def normalize_back(upstream, normed, inv_spread, norm_gain):
    scaled = upstream * norm_gain
    inner_term = (
        scaled
        - jnp.mean(scaled, axis=-1, keepdims=True)
        - normed * jnp.mean(scaled * normed, axis=-1, keepdims=True)
    )
    return (inv_spread * inner_term, jnp.sum(upstream * normed, axis=0), jnp.sum(upstream, axis=0))


def phi_cdf(pre_act):
    return 0.5 * (1.0 + lax.erf(pre_act * ROOT_HALF))


def mm(left, right):
    return jnp.dot(left, right, preferred_element_type=f32)


def mm_nt(left, right):
    return lax.dot_general(left, right, (((1,), (1,)), ((), ())), preferred_element_type=f32)


def mm_tn(left, right):
    return lax.dot_general(left, right, (((0,), (0,)), ((), ())), preferred_element_type=f32)


def swap(value, axis):
    return lax.ppermute(value, axis, [(0, 1), (1, 0)])


def shift(value, axis, steps):
    size = lax.axis_size(axis)
    return lax.ppermute(value, axis, [(i, (i + steps) % size) for i in range(size)])


def pick(value, index, axis):
    return lax.dynamic_index_in_dim(value, index, axis, keepdims=False)


def gather_line(block):
    size = lax.axis_size("z")
    if size > 4:
        return lax.all_gather(block, "z", axis=0)
    place = lax.axis_index("z")
    out = jnp.zeros((size, *block.shape), block.dtype)
    out = lax.dynamic_update_index_in_dim(out, block, place, 0)
    for k in range(1, size):
        out = lax.dynamic_update_index_in_dim(
            out, shift(block, "z", k), lax.rem(place + size - k, size), 0
        )
    return out


def weave(same, other, x):
    first = jnp.where(x == 0, same, other)
    second = jnp.where(x == 0, other, same)
    both = jnp.stack([first, second], axis=1)
    return both.reshape(-1, both.shape[-1])


def spread(block):
    x = lax.axis_index("x")
    line = gather_line(block)
    half = line.shape[0] // 2
    low, high = line[:half], line[half:]
    low_x, high_y = swap(low, "x"), swap(high, "y")
    low_two = swap(jnp.stack([low, low_x]), "y")
    high_two = swap(jnp.stack([high, high_y]), "x")
    own = weave(jnp.concatenate([low, high]), jnp.concatenate([low_x, high_two[0]]), x)
    far = weave(jnp.concatenate([low_two[0], high_y]), jnp.concatenate([low_two[1], high_two[1]]), x)
    return own, far


def collect(own, far, rows):
    x, z = lax.axis_index("x"), lax.axis_index("z")
    size = lax.axis_size("z")
    half = size // 2
    cols = own.shape[1]
    own = own.reshape(size, 2, rows, cols)
    far = far.reshape(size, 2, rows, cols)
    got = swap(
        jnp.stack([pick(own[:half], 1 - x, 1), pick(far[:half], 1 - x, 1)]).astype(bf16), "x"
    ).astype(f32)
    low = pick(own[:half], x, 1) + got[0]
    low_far = pick(far[:half], x, 1) + got[1]
    low = low + swap(low_far.astype(bf16), "y").astype(f32)
    high = own[half:] + swap(far[half:].astype(bf16), "y").astype(f32)
    high = pick(high, x, 1) + swap(pick(high, 1 - x, 1).astype(bf16), "x").astype(f32)
    line = jnp.concatenate([low, high])
    if size > 4:
        return lax.psum_scatter(line, "z", scatter_dimension=0)
    total = pick(line, z, 0)
    for k in range(1, size):
        total = total + shift(pick(line, lax.rem(z + k, size), 0).astype(bf16), "z", k).astype(f32)
    return total


def total_small(value):
    value = value + swap(value, "x")
    value = value + swap(value, "y")
    size = lax.axis_size("z")
    if size > 4:
        return lax.psum(value, "z")
    total = value
    for k in range(1, size):
        total = total + shift(value, "z", k)
    return total


def masked_scores(queries, key_rows, seg_rows, seg_cols):
    scores = jnp.einsum("qhd,khd->hqk", queries, key_rows, preferred_element_type=f32)
    same_doc = seg_rows[:, None] == seg_cols[None, :]
    return jnp.where(same_doc[None, :, :], scores * (1.0 / math.sqrt(HD)), NEG_FILL)


def attend_forward(queries, key_rows, value_rows, segment):
    scores = masked_scores(queries, key_rows, segment, segment)
    row_max = jnp.max(scores, axis=-1, keepdims=True)
    exp_scores = jnp.exp(scores - row_max)
    row_total = jnp.sum(exp_scores, axis=-1, keepdims=True)
    prob_low = (exp_scores / row_total).astype(bf16)
    mixed = jnp.einsum("hqk,khd->qhd", prob_low, value_rows, preferred_element_type=f32)
    return mixed.astype(bf16), row_max + jnp.log(row_total)


def attend_back(queries, key_rows, value_rows, segment, log_rows, grad_rows):
    scale = 1.0 / math.sqrt(HD)
    scores = masked_scores(queries, key_rows, segment, segment)
    probs = jnp.exp(scores - log_rows)
    prob_low = probs.astype(bf16)
    value_grad = jnp.einsum("hqk,qhd->khd", prob_low, grad_rows, preferred_element_type=f32)
    prob_grad = jnp.einsum("qhd,khd->hqk", grad_rows, value_rows, preferred_element_type=f32)
    row_dot = jnp.sum(probs * prob_grad, axis=-1, keepdims=True)
    score_low = (probs * (prob_grad - row_dot)).astype(bf16)
    query_grad = jnp.einsum("hqk,khd->qhd", score_low, key_rows, preferred_element_type=f32) * scale
    key_grad = jnp.einsum("hqk,qhd->khd", score_low, queries, preferred_element_type=f32) * scale
    return query_grad, key_grad, value_grad


def shards(
    tokens,
    segments,
    query_weight,
    query_bias,
    key_weight,
    value_weight,
    value_bias,
    out_weight,
    out_bias,
    attn_gain,
    attn_shift,
    inner_weight,
    inner_bias,
    outer_weight,
    outer_bias,
    ffn_gain,
    ffn_shift,
    out_grad,
):
    share, width = tokens.shape
    rows, head_width = query_weight.shape
    units = inner_weight.shape[1]
    length = segments.shape[1]
    y, core = lax.axis_index("y"), lax.axis_index("c")
    start = core * share
    other_start = (1 - core) * share

    def own_rows(full):
        return lax.dynamic_slice_in_dim(full, start, share, 0)

    def other_rows(full):
        return lax.dynamic_slice_in_dim(full, other_start, share, 0)

    def whole(own):
        other = swap(own, "c")
        return jnp.where(core == 0, jnp.concatenate([own, other]), jnp.concatenate([other, own]))

    def pair_sum(product):
        sent = swap(product(other_rows).astype(bf16), "c")
        return product(own_rows) + sent.astype(f32)

    segment = pick(segments, y, 0)
    biases = jnp.concatenate([query_bias, value_bias, inner_bias])
    far_biases = swap(biases, "y")
    head_weights = jnp.concatenate(
        [query_weight, key_weight, value_weight, out_weight], axis=1
    ).astype(bf16)
    full_tokens = whole(tokens)
    head_own, head_far = spread(head_weights)
    inner_own, inner_far = spread(inner_weight.astype(bf16))
    outer_own, outer_far = spread(outer_weight.astype(bf16))

    def columns(part):
        at = slice(part * head_width, (part + 1) * head_width)
        return jnp.concatenate([head_own[:, at], head_far[:, at]], axis=1)

    query_mat, key_mat, value_mat, out_mat = (columns(part) for part in range(4))
    two_query_bias = jnp.concatenate([biases[:head_width], far_biases[:head_width]])
    two_value_bias = jnp.concatenate(
        [biases[head_width : 2 * head_width], far_biases[head_width : 2 * head_width]]
    )
    inner_mat = jnp.concatenate([inner_own, inner_far], axis=1)
    outer_mat = jnp.concatenate([outer_own, outer_far], axis=1)
    two_inner_bias = jnp.concatenate([biases[2 * head_width :], far_biases[2 * head_width :]])

    query_low = (mm(full_tokens, query_mat) + two_query_bias).astype(bf16)
    key_low = mm(full_tokens, key_mat).astype(bf16)
    value_low = (mm(full_tokens, value_mat) + two_value_bias).astype(bf16)

    def heads_view(flat):
        return flat.reshape(length, -1, HD)

    mixed_heads, log_totals = attend_forward(
        heads_view(query_low), heads_view(key_low), heads_view(value_low), segment
    )
    mixed = mixed_heads.reshape(length, -1)
    attn_total = pair_sum(lambda take: mm_nt(take(mixed), out_mat))
    hidden, normed_one, inv_one = normalize_rows(
        tokens.astype(f32) + attn_total + out_bias, attn_gain, attn_shift
    )
    hidden_low = whole(hidden.astype(bf16))
    inner_pre = mm(hidden_low, inner_mat) + two_inner_bias
    cdf = phi_cdf(inner_pre)
    active_low = (inner_pre * cdf).astype(bf16)
    slope = cdf + inner_pre * jnp.exp(-0.5 * inner_pre * inner_pre) * INV_ROOT_TAU
    ffn_total = pair_sum(lambda take: mm_nt(take(active_low), outer_mat))
    out_full, normed_two, inv_two = normalize_rows(
        hidden + ffn_total + outer_bias, ffn_gain, ffn_shift
    )
    layer_out = out_full.astype(bf16)
    grad_two, ffn_gain_part, ffn_shift_part = normalize_back(
        out_grad.astype(f32), normed_two, inv_two, ffn_gain
    )
    grad_two_low = whole(grad_two.astype(bf16))
    outer_grad_own = mm_tn(grad_two_low, active_low[:, :units])
    outer_grad_far = mm_tn(grad_two_low, active_low[:, units:])
    outer_sum = collect(outer_grad_own, outer_grad_far, rows)
    inner_grad = mm(grad_two_low, outer_mat) * slope
    inner_bias_part = jnp.sum(inner_grad, axis=0)
    inner_low = inner_grad.astype(bf16)
    inner_grad_own = mm_tn(hidden_low, inner_low[:, :units])
    inner_grad_far = mm_tn(hidden_low, inner_low[:, units:])
    inner_sum = collect(inner_grad_own, inner_grad_far, rows)
    back_total = pair_sum(lambda take: mm_nt(take(inner_low), inner_mat))
    grad_one, attn_gain_part, attn_shift_part = normalize_back(
        grad_two + back_total, normed_one, inv_one, attn_gain
    )
    grad_one_low = whole(grad_one.astype(bf16))
    out_w_grad = mm_tn(grad_one_low, mixed)
    mixed_grad = mm(grad_one_low, out_mat).astype(bf16)
    query_grad, key_grad, value_grad = attend_back(
        heads_view(query_low),
        heads_view(key_low),
        heads_view(value_low),
        segment,
        log_totals,
        heads_view(mixed_grad),
    )
    query_grad, key_grad, value_grad = (
        grad.reshape(length, -1) for grad in (query_grad, key_grad, value_grad)
    )
    query_bias_part = jnp.sum(query_grad, axis=0)
    value_bias_part = jnp.sum(value_grad, axis=0)
    query_grad, key_grad, value_grad = (
        grad.astype(bf16) for grad in (query_grad, key_grad, value_grad)
    )
    head_grads = (
        mm_tn(full_tokens, query_grad),
        mm_tn(full_tokens, key_grad),
        mm_tn(full_tokens, value_grad),
        out_w_grad,
    )
    head_sum = collect(
        jnp.concatenate([grad[:, :head_width] for grad in head_grads], axis=1),
        jnp.concatenate([grad[:, head_width:] for grad in head_grads], axis=1),
        rows,
    )
    input_total = pair_sum(
        lambda take: mm_nt(take(query_grad), query_mat)
        + mm_nt(take(key_grad), key_mat)
        + mm_nt(take(value_grad), value_mat)
    )
    tokens_grad = grad_one + input_total
    row_sums = jnp.concatenate(
        [
            jnp.sum(grad_one, axis=0),
            attn_gain_part,
            attn_shift_part,
            jnp.sum(grad_two, axis=0),
            ffn_gain_part,
            ffn_shift_part,
        ]
    )
    row_sums = row_sums + swap(row_sums, "c")

    def in_order(part, size):
        own, far = part[:size], part[size:]
        return jnp.where(y == 0, jnp.concatenate([own, far]), jnp.concatenate([far, own]))

    sums = total_small(
        jnp.concatenate(
            [
                row_sums,
                in_order(query_bias_part, head_width),
                in_order(value_bias_part, head_width),
                in_order(inner_bias_part, units),
            ]
        )
    )
    out_bsum, attn_gsum, attn_ssum, outer_bsum, ffn_gsum, ffn_ssum = (
        sums[i * width : (i + 1) * width] for i in range(6)
    )
    at = 6 * width

    def own_part(begin, size):
        return lax.dynamic_slice_in_dim(sums[begin : begin + 2 * size], y * size, size, 0)

    query_bias_grad = own_part(at, head_width)
    value_bias_grad = own_part(at + 2 * head_width, head_width)
    inner_bias_grad = own_part(at + 4 * head_width, units)
    query_wsum, key_wsum, value_wsum, out_wsum = (
        head_sum[:, part * head_width : (part + 1) * head_width] for part in range(4)
    )
    return (
        layer_out,
        tokens_grad,
        query_wsum,
        query_bias_grad,
        key_wsum,
        value_wsum,
        value_bias_grad,
        out_wsum,
        out_bsum,
        attn_gsum,
        attn_ssum,
        inner_sum,
        inner_bias_grad,
        outer_sum,
        outer_bsum,
        ffn_gsum,
        ffn_ssum,
    )


def solution(mesh):
    groups, tensor = mesh.shape["dp"], mesh.shape["tensor"]
    grid = Mesh(mesh.devices.reshape(groups // 2, 2, tensor // 2, 2), ("z", "x", "y", "c"))
    dp, tp = ("z", "x"), ("y", "c")
    every = ("z", "x", "y", "c")
    in_specs = (
        P(every, None),
        P(dp, None),
        P(dp, tp),
        P(tp),
        P(dp, tp),
        P(dp, tp),
        P(tp),
        P(dp, tp),
        P(),
        P(),
        P(),
        P(dp, tp),
        P(tp),
        P(dp, tp),
        P(),
        P(),
        P(),
        P(every, None),
    )
    out_specs = (
        P(every, None),
        P(every, None),
        P(dp, tp),
        P(tp),
        P(dp, tp),
        P(dp, tp),
        P(tp),
        P(dp, tp),
        P(),
        P(),
        P(),
        P(dp, tp),
        P(tp),
        P(dp, tp),
        P(),
        P(),
        P(),
    )
    return jax.shard_map(shards, mesh=grid, in_specs=in_specs, out_specs=out_specs, check_vma=False)
```

time: 1170 us -> 371 us (0.32)
  waiting for transfers between devices: 720 us -> 71.8 us
  blocking collectives: 170 us -> 0 us
  starting transfers between devices: 0.88 us -> 91.4 us
  matrix products: 154 us -> 115 us
  between operations: 16.5 us -> 2.8 us
    psum x2 -> x0, waiting for transfers between devices: 239 us -> none  [the longest x1 120 us: shards(): ffn_total = lax.psum(ffn_part, 'tensor')]
    reduce_scatter x5 -> x0, waiting for transfers between devices: 226 us -> none  [the longest x1 72.1 us: shards(): lax.psum_scatter(inner_w_grad, 'dp', scatter_dimension=0, tiled=True)]
    unnamed x18 -> x0, waiting for transfers between devices: 198 us -> none
    all_gather x4 -> x0, blocking collectives: 128 us -> none  [the longest x1 33.1 us: shards(): lax.all_gather(value_weight.astype(jnp.bfloat16), 'dp', axis=0, tiled=True)]
    ppermute x0 -> x57, starting transfers between devices: none -> 91.4 us  [the longest x21 61.1 us: shift(): lax.ppermute(value, axis, [(i, (i + steps) % size) for i in range(size)])]
    ppermute x0 -> x57, waiting for transfers between devices: none -> 71.8 us  [the longest x36 54.6 us: swap(): return lax.ppermute(value, axis, [(0, 1), (1, 0)])]
    all_gather x5 -> x0, waiting for transfers between devices: 57.5 us -> none  [the longest x1 28.8 us: shards(): lax.all_gather(grad_two.astype(jnp.bfloat16), 'tensor', axis=0, tiled=True)]
    psum x1 -> x0, blocking collectives: 41.2 us -> none  [shards(): lax.psum((padded(query_bias_part, model_width), padded(value_bias_part, m...]
  transfers between devices with their start and end apart: 15 -> 57, of which waited for: 11 -> 24; matrix products, arithmetic and copies ran while one was open for 6% -> 22% of each run, Pallas kernels for 0% -> 0%
where the time goes in v1:
time: 371 us; the launch traced here: 368 us
  matrix products  115 us (31%)
  starting transfers between devices  91.4 us (25%)
  waiting for transfers between devices  71.8 us (19%)
  other arithmetic  52.6 us (14%)
  local copies, waits for them, and re-layouts  33.9 us (9%)
    ppermute x21, starting transfers between devices, shift(): lax.ppermute(value, axis, [(i, (i + steps) % size) for i in range(size)])  61.1 us
    ppermute x36, waiting for transfers between devices, swap(): return lax.ppermute(value, axis, [(0, 1), (1, 0)])  54.6 us
    ppermute x36, starting transfers between devices, swap(): return lax.ppermute(value, axis, [(0, 1), (1, 0)])  30.3 us
    dot_general x12, matrix products, mm_nt(): lax.dot_general(left, right, (((1,), (1,)), ((), ())), preferred_element_...  20.5 us
    ppermute x21, waiting for transfers between devices, shift(): lax.ppermute(value, axis, [(i, (i + steps) % size) for i in range(size)])  17.2 us
    dot_general x6, matrix products, mm(): return jnp.dot(left, right, preferred_element_type=f32)  17 us
    convert_element_type x1, other arithmetic, attend_back(): score_low = (probs * (prob_grad - row_dot)).astype(bf16)  16.9 us
    dot_general x1, matrix products, attend_back(): jnp.einsum('qhd,khd->hqk', grad_rows, value_rows, preferred_element_type=...  16.1 us
  transfers between devices with their start and end apart: 57, of which 24 were waited for; matrix products, arithmetic and copies ran while one was open for 22% of the time, Pallas kernels for 0%

profile of v1, /device:TPU:0, one launch (start us, length us, event | category | flops | bytes accessed | tf_op | source)
XLA Modules:
  0.0 367.8 jit_solution(10435842619872011840)
XLA Ops:
  5.2 3.0 collective-permute-start.1
  8.2 2.6 collective-permute-start.2
  18.3 2.9 collective-permute-start.13
  22.1 8.0 %collective-permute-start.18 = (bf16[96,768]{1,0:T(8,128)(2,1)}, bf16[96,768]{1,0:T(8,128)(2,1)S(1)}, u32[]{:S(2)}, u32[]{:S(2)}) collective-permute-start(bf16[96,768]{1,0:T(8,128)(2,1)} %get-tuple-element.30), channel_id=1, source_target_pairs={{0,8},{8,16},{16,24},{24,0},{1,9},{9,17},{17,25},{25,1},{2,10},{10... | collective-permute-start | bytes 442376 | tf_op jit(solution)/shard_map/ppermute | solution.py:56
  30.1 3.5 collective-permute-start.19
  34.4 3.8 %collective-permute-done.12 = bf16[96,768]{1,0:T(8,128)(2,1)S(1)} collective-permute-done((bf16[96,768]{1,0:T(8,128)(2,1)}, bf16[96,768]{1,0:T(8,128)(2,1)S(1)}, u32[]{:S(2)}, u32[]{:S(2)}) %collective-permute-start.12) | collective-permute-done | bytes 147488 | tf_op jit(solution)/shard_map/ppermute | solution.py:56
  38.3 1.7 collective-permute-start.5
  40.1 1.6 collective-permute-start.4
  41.6 4.3 %collective-permute-done.19 = bf16[96,768]{1,0:T(8,128)(2,1)S(1)} collective-permute-done((bf16[96,768]{1,0:T(8,128)(2,1)}, bf16[96,768]{1,0:T(8,128)(2,1)S(1)}, u32[]{:S(2)}, u32[]{:S(2)}) %collective-permute-start.19) | collective-permute-done | bytes 147488 | tf_op jit(solution)/shard_map/ppermute | solution.py:56
  46.0 1.5 collective-permute-start.15
  47.5 1.6 collective-permute-start.14
  49.9 1.6 collective-permute-start.6
  51.5 3.3 collective-permute-done.15
  54.8 1.5 collective-permute-start.22
  58.1 5.8 %collective-permute-done.21 = bf16[2,96,768]{2,1,0:T(8,128)(2,1)S(1)} collective-permute-done((bf16[2,96,768]{2,1,0:T(8,128)(2,1)S(1)}, bf16[2,96,768]{2,1,0:T(8,128)(2,1)S(1)}, u32[]{:S(2)}, u32[]{:S(2)}) %collective-permute-start.21) | collective-permute-done | bytes 294944 | tf_op jit(solution)/shard_map/ppermute | solution.py:51
  66.3 10.1 %collective-permute-done.6 = bf16[2,2,96,768]{3,2,1,0:T(8,128)(2,1)S(1)} collective-permute-done((bf16[2,2,96,768]{3,2,1,0:T(8,128)(2,1)S(1)}, bf16[2,2,96,768]{3,2,1,0:T(8,128)(2,1)S(1)}, u32[]{:S(2)}, u32[]{:S(2)}) %collective-permute-start.6) | collective-permute-done | bytes 589856 | tf_op jit(solution)/shard_map/ppermute | solution.py:51
  82.6 10.7 %fusion.169 = (f32[6,1024]{1,0:T(8,128)S(1)}, f32[6,1024,1024]{1,2,0:T(8,128)}) fusion(bf16[1024,6,64]{0,2,1:T(8,128)(2,1)S(1)} %bitcast.276, bf16[1024,6,64]{0,2,1:T(8,128)(2,1)S(1)} %bitcast.278, pred[1024,1024]{0,1:T(8,128)(4,1)S(1)} %broadcast_compare_fusion), kind=kOutput, calls=%fused_computation.347 | convolution fusion | flops 824174592 | bytes 27811840 | tf_op jit(solution)/shard_map/qhd,khd->hqk/dot_general | solution.py:134
  93.3 10.2 %fusion = f32[6,1024]{1,0:T(8,128)S(1)} fusion(f32[6,1024,1024]{1,2,0:T(8,128)} %get-tuple-element.124, f32[6,1024]{1,0:T(8,128)S(1)} %get-tuple-element.123), kind=kLoop, calls=%fused_computation.6 | loop fusion | flops 12576768 | bytes 25214976 | tf_op jit(solution)/shard_map/reduce_sum | solution.py:143
  104.5 11.4 %fusion.40 = bf16[6,64,1024]{2,1,0:T(8,128)(2,1)S(1)} fusion(bf16[1024,6,64]{0,2,1:T(8,128)(2,1)S(1)} %bitcast.330, f32[6,1024,1024]{1,2,0:T(8,128)} %get-tuple-element.124, f32[6,1024]{1,0:T(8,128)S(1)} %fusion, f32[6,1024]{1,0:T(8,128)S(1)} %get-tuple-element.123), kind=kOutput, calls=%fused_computation.105 | convolution fusion | flops 824573952 | bytes 26787840 | tf_op jit(solution)/shard_map/hqk,khd->qhd/dot_general | solution.py:145
  117.3 1.7 collective-permute-done.9
  123.4 5.5 %multiply_convert_fusion.1 = (bf16[1024,1536]{1,0:T(8,128)(2,1)S(1)}, f32[1024,1536]{1,0:T(8,128)}) fusion(f32[1536]{0:T(1024)S(1)} %pad_maximum_fusion.40, bf16[768,768]{1,0:T(8,128)(2,1)S(1)} %bitcast.321, bf16[768,768]{1,0:T(8,128)(2,1)S(1)} %bitcast.318, bf16[512,768]{1,0:T(8,128)(2,1)S(1)} %collective-permute-done.10, ...), kind=kOutput, calls=%fused_computation.17 | convolution fusion | flops 2437152768 | bytes 13375489 | tf_op jit(solution)/shard_map/dot_general | solution.py:39
  130.5 2.2 collective-permute-done.25
  132.7 1.7 fusion.171
  136.9 2.1 fusion.149
  142.7 3.8 %fusion.18 = f32[768,768]{1,0:T(8,128)S(1)} fusion(bf16[1024,1536]{1,0:T(8,128)(2,1)} %copy-done.83, bf16[512,768]{1,0:T(8,128)(2,1)} %collective-permute-done.26, bf16[512,768]{1,0:T(8,128)(2,1)} %convert_element_type.286, pred[]{:T(512)S(6)} %eq.18), kind=kOutput, calls=%fused_computation.58 | convolution fusion | flops 1215037440 | bytes 5505025 | tf_op jit(solution)/shard_map/dot_general | solution.py:47
  148.1 7.9 %fusion.152 = (f32[1536]{0:T(1024)S(1)}, bf16[1024,1536]{1,0:T(8,128)(2,1)S(1)}) fusion(f32[1024,1536]{1,0:T(8,128)} %get-tuple-element.128, f32[1536]{0:T(1024)S(1)} %copy-done.70, bf16[768,768]{1,0:T(8,128)(2,1)S(1)} %bitcast.326, bf16[768,768]{1,0:T(8,128)(2,1)S(1)} %bitcast.329, bf16[512,768]{1,0:T(8,128)(2,1)} %collective-permute-done.26, ...), kind=kOutput, calls=%fused_computation.330 | convolution fusion | flops 2446588416 | bytes 13381633 | tf_op jit(solution)/shard_map/dot_general | solution.py:39
  156.0 1.5 fusion.22
  157.7 1.7 copy-done.84
  159.5 3.4 fusion.20
  163.1 1.6 collective-permute-start.52
  167.9 1.6 collective-permute-start.43
  171.0 8.3 %collective-permute-done.52 = bf16[2,2,96,768]{3,2,0,1:T(8,128)(2,1)S(1)} collective-permute-done((bf16[2,2,96,768]{3,2,0,1:T(8,128)(2,1)S(1)}, bf16[2,2,96,768]{3,2,0,1:T(8,128)(2,1)S(1)}, u32[]{:S(2)}, u32[]{:S(2)}) %collective-permute-start.52) | collective-permute-done | bytes 589856 | tf_op jit(solution)/shard_map/ppermute | solution.py:51
  181.9 10.1 %collective-permute-done.45 = bf16[2,2,96,768]{3,2,0,1:T(8,128)(2,1)S(1)} collective-permute-done((bf16[2,2,96,768]{3,2,0,1:T(8,128)(2,1)S(1)}, bf16[2,2,96,768]{3,2,0,1:T(8,128)(2,1)S(1)}, u32[]{:S(2)}, u32[]{:S(2)}) %collective-permute-start.45) | collective-permute-done | bytes 589856 | tf_op jit(solution)/shard_map/ppermute | solution.py:51
  193.9 2.0 multiply_reduce_fusion.1
  200.3 3.9 %collective-permute-start.54 = (bf16[96,768]{1,0:T(8,128)(2,1)S(1)}, bf16[96,768]{1,0:T(8,128)(2,1)S(1)}, u32[]{:S(2)}, u32[]{:S(2)}) collective-permute-start(bf16[96,768]{1,0:T(8,128)(2,1)S(1)} %get-tuple-element.42), channel_id=1, source_target_pairs={{0,8},{8,16},{16,24},{24,0},{1,9},{9,17},{17,25},{25,1},{2,10},{10... | collective-permute-start | bytes 442376 | tf_op jit(solution)/shard_map/ppermute | solution.py:56
  204.2 3.2 collective-permute-start.55
  207.5 5.4 %collective-permute-start.56 = (bf16[96,768]{1,0:T(8,128)(2,1)S(1)}, bf16[96,768]{1,0:T(8,128)(2,1)S(1)}, u32[]{:S(2)}, u32[]{:S(2)}) collective-permute-start(bf16[96,768]{1,0:T(8,128)(2,1)S(1)} %get-tuple-element.44), channel_id=1, source_target_pairs={{0,24},{8,0},{16,8},{24,16},{1,25},{9,1},{17,9},{25,17},{2,26},{10... | collective-permute-start | bytes 442376 | tf_op jit(solution)/shard_map/ppermute | solution.py:56
  213.3 5.3 %collective-permute-start.48 = (bf16[96,768]{1,0:T(8,128)(2,1)S(1)}, bf16[96,768]{1,0:T(8,128)(2,1)S(1)}, u32[]{:S(2)}, u32[]{:S(2)}) collective-permute-start(bf16[96,768]{1,0:T(8,128)(2,1)S(1)} %get-tuple-element.46), channel_id=1, source_target_pairs={{0,16},{8,24},{16,0},{24,8},{1,17},{9,25},{17,1},{25,9},{2,18},{10... | collective-permute-start | bytes 442376 | tf_op jit(solution)/shard_map/ppermute | solution.py:56
  218.6 10.1 %collective-permute-start.49 = (bf16[96,768]{1,0:T(8,128)(2,1)S(1)}, bf16[96,768]{1,0:T(8,128)(2,1)S(1)}, u32[]{:S(2)}, u32[]{:S(2)}) collective-permute-start(bf16[96,768]{1,0:T(8,128)(2,1)S(1)} %get-tuple-element.47), channel_id=1, source_target_pairs={{0,24},{8,0},{16,8},{24,16},{1,25},{9,1},{17,9},{25,17},{2,26},{10... | collective-permute-start | bytes 442376 | tf_op jit(solution)/shard_map/ppermute | solution.py:56
  229.6 1.8 collective-permute-done.49
  233.2 16.1 %multiply_reduce_fusion = (f32[6,1024]{1,0:T(8,128)S(1)}, f32[6,1024,1024]{1,2,0:T(8,128)}) fusion(f32[6,1024,1024]{1,2,0:T(8,128)} %get-tuple-element.124, f32[6,1024]{1,0:T(8,128)S(1)} %copy-done.48, bf16[1024,6,64]{0,2,1:T(8,128)(2,1)S(1)} %bitcast.298, bf16[1024,6,64]{0,2,1:T(8,128)(2,1)} %bitcast.331), kind=kOutput, calls=%fused_computation.1 | convolution fusion | flops 824174592 | bytes 51953664 | tf_op jit(solution)/shard_map/qhd,khd->hqk/dot_general | solution.py:155
  249.4 16.9 %multiply_convert_fusion = bf16[6,1024,1024]{1,2,0:T(8,128)(2,1)S(1)} fusion(f32[6,1024,1024]{1,2,0:T(8,128)} %get-tuple-element.134, f32[6,1024,1024]{1,2,0:T(8,128)} %get-tuple-element.124, f32[6,1024]{1,0:T(8,128)S(1)} %get-tuple-element.133, f32[6,1024]{1,0:T(8,128)S(1)} %copy-done.48), kind=kLoop, calls=%fused_computation | loop fusion | flops 25165824 | bytes 62963712 | tf_op jit(solution)/shard_map/convert_element_type | solution.py:157
  266.3 3.9 %bitcast_convert_fusion.1 = (bf16[1024,6,64]{0,2,1:T(8,128)(2,1)}, f32[6,64,1024]{2,1,0:T(8,128)S(1)}) fusion(bf16[1024,6,64]{0,2,1:T(8,128)(2,1)S(1)} %bitcast.279, bf16[6,1024,1024]{1,2,0:T(8,128)(2,1)S(1)} %multiply_convert_fusion), kind=kOutput, calls=%fused_computation.73 | convolution fusion | flops 806092800 | bytes 15728640 | tf_op jit(solution)/shard_map/hqk,khd->qhd/dot_general | solution.py:158
  271.7 13.3 %bitcast_convert_fusion = (bf16[1024,6,64]{0,2,1:T(8,128)(2,1)}, f32[6,64,1024]{2,1,0:T(8,128)S(1)}) fusion(bf16[1024,6,64]{0,2,1:T(8,128)(2,1)} %bitcast.299, f32[6,1024,1024]{1,2,0:T(8,128)} %get-tuple-element.124, f32[6,1024]{1,0:T(8,128)S(1)} %copy-done.49), kind=kOutput, calls=%fused_computation.71 | convolution fusion | flops 818282496 | bytes 28336128 | tf_op jit(solution)/shard_map/hqk,qhd->khd/dot_general | solution.py:154
  285.3 8.9 %multiply_convert_fusion.2 = bf16[6,64,1024]{2,1,0:T(8,128)(2,1)S(1)} fusion(bf16[1024,6,64]{0,2,1:T(8,128)(2,1)} %bitcast.277, bf16[6,1024,1024]{1,2,0:T(8,128)(2,1)} %copy-done.2), kind=kOutput, calls=%fused_computation.77 | convolution fusion | flops 806092800 | bytes 14155776 | tf_op jit(solution)/shard_map/hqk,qhd->khd/dot_general | solution.py:159
  303.5 2.1 fusion.65
  305.6 1.9 fusion.67
  307.5 2.0 fusion.60
  309.5 1.9 fusion.62
  313.9 1.6 fusion.155
  316.6 2.0 collective-permute-start.32
  318.6 2.6 copy.63
  321.3 1.8 fusion.74
  324.5 1.8 fusion.78
  326.3 2.8 copy.66
  331.2 2.0 collective-permute-start.30
  335.3 3.5 collective-permute-start.41
  338.8 2.2 add_convert_fusion
  348.8 3.7 %collective-permute-done.33 = bf16[2,96,768]{2,1,0:T(8,128)(2,1)S(1)} collective-permute-done((bf16[2,96,768]{2,1,0:T(8,128)(2,1)S(1)}, bf16[2,96,768]{2,1,0:T(8,128)(2,1)S(1)}, u32[]{:S(2)}, u32[]{:S(2)}) %collective-permute-start.33) | collective-permute-done | bytes 294944 | tf_op jit(solution)/shard_map/ppermute | solution.py:51
  354.1 2.1 collective-permute-start.34
  356.2 2.8 collective-permute-start.35
  359.0 2.1 add_add_fusion
  361.1 1.6 collective-permute-done.34
  362.8 3.9 %collective-permute-done.35 = bf16[96,768]{1,0:T(8,128)(2,1)S(1)} collective-permute-done((bf16[96,768]{1,0:T(8,128)(2,1)S(1)}, bf16[96,768]{1,0:T(8,128)(2,1)S(1)}, u32[]{:S(2)}, u32[]{:S(2)}) %collective-permute-start.35) | collective-permute-done | bytes 147488 | tf_op jit(solution)/shard_map/ppermute | solution.py:56
  (423 shorter events, 87.1 us)
Async XLA Ops:
  5.2 13.1 %collective-permute-start.1 = (bf16[96,768]{1,0:T(8,128)(2,1)}, bf16[96,768]{1,0:T(8,128)(2,1)}, u32[]{:S(2)}, u32[]{:S(2)}) collective-permute-start(bf16[96,768]{1,0:T(8,128)(2,1)} %pad_maximum_fusion.38), channel_id=1, source_target_pairs={{0,8},{8,16},{16,24},{24,0},{1,9},{9,17},{17,25},{25,1},{2,10},{10... | collective-permute-start | bytes 442376 | tf_op jit(solution)/shard_map/ppermute | solution.py:56
  8.2 13.9 %collective-permute-start.2 = (bf16[96,768]{1,0:T(8,128)(2,1)}, bf16[96,768]{1,0:T(8,128)(2,1)S(1)}, u32[]{:S(2)}, u32[]{:S(2)}) collective-permute-start(bf16[96,768]{1,0:T(8,128)(2,1)} %pad_maximum_fusion.38), channel_id=1, source_target_pairs={{0,16},{8,24},{16,0},{24,8},{1,17},{9,25},{17,1},{25,9},{2,18},{10... | collective-permute-start | bytes 442376 | tf_op jit(solution)/shard_map/ppermute | solution.py:56
  10.8 19.3 %collective-permute-start.3 = (bf16[96,768]{1,0:T(8,128)(2,1)}, bf16[96,768]{1,0:T(8,128)(2,1)S(1)}, u32[]{:S(2)}, u32[]{:S(2)}) collective-permute-start(bf16[96,768]{1,0:T(8,128)(2,1)} %pad_maximum_fusion.38), channel_id=1, source_target_pairs={{0,24},{8,0},{16,8},{24,16},{1,25},{9,1},{17,9},{25,17},{2,26},{10... | collective-permute-start | bytes 442376 | tf_op jit(solution)/shard_map/ppermute | solution.py:56
  12.9 4.7 %collective-permute-start.8 = (f32[1152]{0:T(1024)S(1)}, f32[1152]{0:T(1024)S(1)}, u32[]{:S(2)}, u32[]{:S(2)}) collective-permute-start(f32[1152]{0:T(1024)S(1)} %concatenate.263), channel_id=1, source_target_pairs={{0,2},{2,0},{1,3},{3,1},{4,6},{6,4},{5,7},{7,5},{8,10},{10,8},{9,1... | collective-permute-start | bytes 13832 | tf_op jit(solution)/shard_map/ppermute | solution.py:51
  15.2 18.5 %collective-permute-start.11 = (bf16[96,768]{1,0:T(8,128)(2,1)}, bf16[96,768]{1,0:T(8,128)(2,1)S(1)}, u32[]{:S(2)}, u32[]{:S(2)}) collective-permute-start(bf16[96,768]{1,0:T(8,128)(2,1)} %get-tuple-element.32), channel_id=1, source_target_pairs={{0,8},{8,16},{16,24},{24,0},{1,9},{9,17},{17,25},{25,1},{2,10},{10... | collective-permute-start | bytes 442376 | tf_op jit(solution)/shard_map/ppermute | solution.py:56
  17.6 20.6 %copy-start.41 = (bf16[512,768]{1,0:T(8,128)(2,1)S(1)}, bf16[512,768]{1,0:T(8,128)(2,1)}, u32[]{:S(2)}) copy-start(bf16[512,768]{1,0:T(8,128)(2,1)} %param.18) | copy-start | bytes 2359300
  17.7 20.6 %collective-permute-start.12 = (bf16[96,768]{1,0:T(8,128)(2,1)}, bf16[96,768]{1,0:T(8,128)(2,1)S(1)}, u32[]{:S(2)}, u32[]{:S(2)}) collective-permute-start(bf16[96,768]{1,0:T(8,128)(2,1)} %get-tuple-element.32), channel_id=1, source_target_pairs={{0,16},{8,24},{16,0},{24,8},{1,17},{9,25},{17,1},{25,9},{2,18},{10... | collective-permute-start | bytes 442376 | tf_op jit(solution)/shard_map/ppermute | solution.py:56
  18.2 105.1 %copy-start.69 = (f32[1536]{0:T(1024)}, f32[1536]{0:T(1024)S(1)}, u32[]{:S(2)}) copy-start(f32[1536]{0:T(1024)S(1)} %pad_maximum_fusion.40) | copy-start | bytes 18436
  18.3 20.0 %collective-permute-start.13 = (bf16[96,768]{1,0:T(8,128)(2,1)}, bf16[96,768]{1,0:T(8,128)(2,1)S(1)}, u32[]{:S(2)}, u32[]{:S(2)}) collective-permute-start(bf16[96,768]{1,0:T(8,128)(2,1)} %get-tuple-element.32), channel_id=1, source_target_pairs={{0,24},{8,0},{16,8},{24,16},{1,25},{9,1},{17,9},{25,17},{2,26},{10... | collective-permute-start | bytes 442376 | tf_op jit(solution)/shard_map/ppermute | solution.py:56
  22.1 18.0 %collective-permute-start.18 = (bf16[96,768]{1,0:T(8,128)(2,1)}, bf16[96,768]{1,0:T(8,128)(2,1)S(1)}, u32[]{:S(2)}, u32[]{:S(2)}) collective-permute-start(bf16[96,768]{1,0:T(8,128)(2,1)} %get-tuple-element.30), channel_id=1, source_target_pairs={{0,8},{8,16},{16,24},{24,0},{1,9},{9,17},{17,25},{25,1},{2,10},{10... | collective-permute-start | bytes 442376 | tf_op jit(solution)/shard_map/ppermute | solution.py:56
  30.1 15.9 %collective-permute-start.19 = (bf16[96,768]{1,0:T(8,128)(2,1)}, bf16[96,768]{1,0:T(8,128)(2,1)S(1)}, u32[]{:S(2)}, u32[]{:S(2)}) collective-permute-start(bf16[96,768]{1,0:T(8,128)(2,1)} %get-tuple-element.30), channel_id=1, source_target_pairs={{0,16},{8,24},{16,0},{24,8},{1,17},{9,25},{17,1},{25,9},{2,18},{10... | collective-permute-start | bytes 442376 | tf_op jit(solution)/shard_map/ppermute | solution.py:56
  33.7 13.8 %collective-permute-start.20 = (bf16[96,768]{1,0:T(8,128)(2,1)}, bf16[96,768]{1,0:T(8,128)(2,1)S(1)}, u32[]{:S(2)}, u32[]{:S(2)}) collective-permute-start(bf16[96,768]{1,0:T(8,128)(2,1)} %get-tuple-element.30), channel_id=1, source_target_pairs={{0,24},{8,0},{16,8},{24,16},{1,25},{9,1},{17,9},{25,17},{2,26},{10... | collective-permute-start | bytes 442376 | tf_op jit(solution)/shard_map/ppermute | solution.py:56
  38.3 42.0 %collective-permute-start = (bf16[512,768]{1,0:T(8,128)(2,1)S(1)}, bf16[512,768]{1,0:T(8,128)(2,1)S(1)}, u32[]{:S(2)}, u32[]{:S(2)}) collective-permute-start(bf16[512,768]{1,0:T(8,128)(2,1)S(1)} %copy-done.41), channel_id=1, source_target_pairs={{0,1},{1,0},{2,3},{3,2},{4,5},{5,4},{6,7},{7,6},{8,9},{9,8},{10,11... | collective-permute-start | bytes 2359304 | tf_op jit(solution)/shard_map/ppermute | solution.py:51
  38.3 10.9 %collective-permute-start.5 = (bf16[2,96,768]{2,1,0:T(8,128)(2,1)S(1)}, bf16[2,96,768]{2,1,0:T(8,128)(2,1)S(1)}, u32[]{:S(2)}, u32[]{:S(2)}) collective-permute-start(bf16[2,96,768]{2,1,0:T(8,128)(2,1)S(1)} %get-tuple-element.93), channel_id=1, source_target_pairs={{0,2},{2,0},{1,3},{3,1},{4,6},{6,4},{5,7},{7,5},{8,10},{10,8},{9,1... | collective-permute-start | bytes 884744 | tf_op jit(solution)/shard_map/ppermute | solution.py:51
  40.1 9.8 %collective-permute-start.4 = (bf16[2,96,768]{2,1,0:T(8,128)(2,1)S(1)}, bf16[2,96,768]{2,1,0:T(8,128)(2,1)S(1)}, u32[]{:S(2)}, u32[]{:S(2)}) collective-permute-start(bf16[2,96,768]{2,1,0:T(8,128)(2,1)S(1)} %get-tuple-element.94), channel_id=1, source_target_pairs={{0,4},{4,0},{1,5},{5,1},{2,6},{6,2},{3,7},{7,3},{8,12},{12,8},{9,1... | collective-permute-start | bytes 884744 | tf_op jit(solution)/shard_map/ppermute | solution.py:51
  46.0 8.8 %collective-permute-start.15 = (bf16[2,96,768]{2,1,0:T(8,128)(2,1)S(1)}, bf16[2,96,768]{2,1,0:T(8,128)(2,1)S(1)}, u32[]{:S(2)}, u32[]{:S(2)}) collective-permute-start(bf16[2,96,768]{2,1,0:T(8,128)(2,1)S(1)} %get-tuple-element.101), channel_id=1, source_target_pairs={{0,2},{2,0},{1,3},{3,1},{4,6},{6,4},{5,7},{7,5},{8,10},{10,8},{9,1... | collective-permute-start | bytes 884744 | tf_op jit(solution)/shard_map/ppermute | solution.py:51
  47.5 10.0 %collective-permute-start.14 = (bf16[2,96,768]{2,1,0:T(8,128)(2,1)S(1)}, bf16[2,96,768]{2,1,0:T(8,128)(2,1)S(1)}, u32[]{:S(2)}, u32[]{:S(2)}) collective-permute-start(bf16[2,96,768]{2,1,0:T(8,128)(2,1)S(1)} %get-tuple-element.102), channel_id=1, source_target_pairs={{0,4},{4,0},{1,5},{5,1},{2,6},{6,2},{3,7},{7,3},{8,12},{12,8},{9,1... | collective-permute-start | bytes 884744 | tf_op jit(solution)/shard_map/ppermute | solution.py:51
  49.2 14.6 %collective-permute-start.21 = (bf16[2,96,768]{2,1,0:T(8,128)(2,1)S(1)}, bf16[2,96,768]{2,1,0:T(8,128)(2,1)S(1)}, u32[]{:S(2)}, u32[]{:S(2)}) collective-permute-start(bf16[2,96,768]{2,1,0:T(8,128)(2,1)S(1)} %get-tuple-element.86), channel_id=1, source_target_pairs={{0,4},{4,0},{1,5},{5,1},{2,6},{6,2},{3,7},{7,3},{8,12},{12,8},{9,1... | collective-permute-start | bytes 884744 | tf_op jit(solution)/shard_map/ppermute | solution.py:51
  49.9 26.6 %collective-permute-start.6 = (bf16[2,2,96,768]{3,2,1,0:T(8,128)(2,1)S(1)}, bf16[2,2,96,768]{3,2,1,0:T(8,128)(2,1)S(1)}, u32[]{:S(2)}, u32[]{:S(2)}) collective-permute-start(bf16[2,2,96,768]{3,2,1,0:T(8,128)(2,1)S(1)} %pad_maximum_fusion.16), channel_id=1, source_target_pairs={{0,4},{4,0},{1,5},{5,1},{2,6},{6,2},{3,7},{7,3},{8,12},{12,8},{9,1... | collective-permute-start | bytes 1769480 | tf_op jit(solution)/shard_map/ppermute | solution.py:51
  54.8 10.6 %collective-permute-start.22 = (bf16[2,96,768]{2,1,0:T(8,128)(2,1)S(1)}, bf16[2,96,768]{2,1,0:T(8,128)(2,1)S(1)}, u32[]{:S(2)}, u32[]{:S(2)}) collective-permute-start(bf16[2,96,768]{2,1,0:T(8,128)(2,1)S(1)} %get-tuple-element.85), channel_id=1, source_target_pairs={{0,2},{2,0},{1,3},{3,1},{4,6},{6,4},{5,7},{7,5},{8,10},{10,8},{9,1... | collective-permute-start | bytes 884744 | tf_op jit(solution)/shard_map/ppermute | solution.py:51
  57.5 19.9 %collective-permute-start.7 = (bf16[2,2,96,768]{3,2,1,0:T(8,128)(2,1)S(1)}, bf16[2,2,96,768]{3,2,1,0:T(8,128)(2,1)S(1)}, u32[]{:S(2)}, u32[]{:S(2)}) collective-permute-start(bf16[2,2,96,768]{3,2,1,0:T(8,128)(2,1)S(1)} %pad_maximum_fusion.18), channel_id=1, source_target_pairs={{0,2},{2,0},{1,3},{3,1},{4,6},{6,4},{5,7},{7,5},{8,10},{10,8},{9,1... | collective-permute-start | bytes 1769480 | tf_op jit(solution)/shard_map/ppermute | solution.py:51
  63.8 52.9 %collective-permute-start.16 = (bf16[2,2,96,768]{3,2,1,0:T(8,128)(2,1)S(1)}, bf16[2,2,96,768]{3,2,1,0:T(8,128)(2,1)S(1)}, u32[]{:S(2)}, u32[]{:S(2)}) collective-permute-start(bf16[2,2,96,768]{3,2,1,0:T(8,128)(2,1)S(1)} %pad_maximum_fusion.25), channel_id=1, source_target_pairs={{0,4},{4,0},{1,5},{5,1},{2,6},{6,2},{3,7},{7,3},{8,12},{12,8},{9,1... | collective-permute-start | bytes 1769480 | tf_op jit(solution)/shard_map/ppermute | solution.py:51
  65.4 51.8 %collective-permute-start.17 = (bf16[2,2,96,768]{3,2,1,0:T(8,128)(2,1)S(1)}, bf16[2,2,96,768]{3,2,1,0:T(8,128)(2,1)S(1)}, u32[]{:S(2)}, u32[]{:S(2)}) collective-permute-start(bf16[2,2,96,768]{3,2,1,0:T(8,128)(2,1)S(1)} %pad_maximum_fusion.27), channel_id=1, source_target_pairs={{0,2},{2,0},{1,3},{3,1},{4,6},{6,4},{5,7},{7,5},{8,10},{10,8},{9,1... | collective-permute-start | bytes 1769480 | tf_op jit(solution)/shard_map/ppermute | solution.py:51
  76.5 40.7 %collective-permute-start.24 = (bf16[2,2,96,768]{3,2,1,0:T(8,128)(2,1)S(1)}, bf16[2,2,96,768]{3,2,1,0:T(8,128)(2,1)S(1)}, u32[]{:S(2)}, u32[]{:S(2)}) collective-permute-start(bf16[2,2,96,768]{3,2,1,0:T(8,128)(2,1)S(1)} %pad_maximum_fusion.32), channel_id=1, source_target_pairs={{0,2},{2,0},{1,3},{3,1},{4,6},{6,4},{5,7},{7,5},{8,10},{10,8},{9,1... | collective-permute-start | bytes 1769480 | tf_op jit(solution)/shard_map/ppermute | solution.py:51
  77.4 39.7 %collective-permute-start.23 = (bf16[2,2,96,768]{3,2,1,0:T(8,128)(2,1)S(1)}, bf16[2,2,96,768]{3,2,1,0:T(8,128)(2,1)S(1)}, u32[]{:S(2)}, u32[]{:S(2)}) collective-permute-start(bf16[2,2,96,768]{3,2,1,0:T(8,128)(2,1)S(1)} %pad_maximum_fusion.30), channel_id=1, source_target_pairs={{0,4},{4,0},{1,5},{5,1},{2,6},{6,2},{3,7},{7,3},{8,12},{12,8},{9,1... | collective-permute-start | bytes 1769480 | tf_op jit(solution)/shard_map/ppermute | solution.py:51
  80.3 23.3 %copy-start.13 = (bf16[768,192]{1,0:T(8,128)(2,1)}, bf16[768,192]{1,0:T(8,128)(2,1)S(1)}, u32[]{:S(2)}) copy-start(bf16[768,192]{1,0:T(8,128)(2,1)S(1)} %get-tuple-element.66) | copy-start | bytes 884740
  80.3 23.3 %copy-start.15 = (bf16[768,192]{1,0:T(8,128)(2,1)}, bf16[768,192]{1,0:T(8,128)(2,1)S(1)}, u32[]{:S(2)}) copy-start(bf16[768,192]{1,0:T(8,128)(2,1)S(1)} %get-tuple-element.143) | copy-start | bytes 884740
  80.3 38.7 %copy-start.31 = (bf16[768,192]{1,0:T(8,128)(2,1)}, bf16[768,192]{1,0:T(8,128)(2,1)S(1)}, u32[]{:S(2)}) copy-start(bf16[768,192]{1,0:T(8,128)(2,1)S(1)} %get-tuple-element.146) | copy-start | bytes 884740
  80.3 23.3 %copy-start.76 = (bf16[512,768]{1,0:T(8,128)(2,1)}, bf16[512,768]{1,0:T(8,128)(2,1)S(1)}, u32[]{:S(2)}) copy-start(bf16[512,768]{1,0:T(8,128)(2,1)S(1)} %collective-permute-done) | copy-start | bytes 2359300
  116.6 2.4 collective-permute-start.9
  121.0 2.4 collective-permute-start.10
  130.4 2.4 collective-permute-start.25
  140.0 2.6 collective-permute-start.26
  163.1 16.2 %collective-permute-start.52 = (bf16[2,2,96,768]{3,2,0,1:T(8,128)(2,1)S(1)}, bf16[2,2,96,768]{3,2,0,1:T(8,128)(2,1)S(1)}, u32[]{:S(2)}, u32[]{:S(2)}) collective-permute-start(bf16[2,2,96,768]{3,2,0,1:T(8,128)(2,1)S(1)} %copy.76), channel_id=1, source_target_pairs={{0,2},{2,0},{1,3},{3,1},{4,6},{6,4},{5,7},{7,5},{8,10},{10,8},{9,1... | collective-permute-start | bytes 1769480 | tf_op jit(solution)/shard_map/ppermute | solution.py:51
  164.8 16.3 %collective-permute-start.50 = (bf16[2,2,96,768]{3,2,1,0:T(8,128)(2,1)S(1)}, bf16[2,2,96,768]{3,2,1,0:T(8,128)(2,1)S(1)}, u32[]{:S(2)}, u32[]{:S(2)}) collective-permute-start(bf16[2,2,96,768]{3,2,1,0:T(8,128)(2,1)S(1)} %pad_maximum_fusion.37), channel_id=1, source_target_pairs={{0,4},{4,0},{1,5},{5,1},{2,6},{6,2},{3,7},{7,3},{8,12},{12,8},{9,1... | collective-permute-start | bytes 1769480 | tf_op jit(solution)/shard_map/ppermute | solution.py:51
  167.2 24.8 %collective-permute-start.45 = (bf16[2,2,96,768]{3,2,0,1:T(8,128)(2,1)S(1)}, bf16[2,2,96,768]{3,2,0,1:T(8,128)(2,1)S(1)}, u32[]{:S(2)}, u32[]{:S(2)}) collective-permute-start(bf16[2,2,96,768]{3,2,0,1:T(8,128)(2,1)S(1)} %copy.72), channel_id=1, source_target_pairs={{0,2},{2,0},{1,3},{3,1},{4,6},{6,4},{5,7},{7,5},{8,10},{10,8},{9,1... | collective-permute-start | bytes 1769480 | tf_op jit(solution)/shard_map/ppermute | solution.py:51
  167.9 25.8 %collective-permute-start.43 = (bf16[2,2,96,768]{3,2,1,0:T(8,128)(2,1)S(1)}, bf16[2,2,96,768]{3,2,1,0:T(8,128)(2,1)S(1)}, u32[]{:S(2)}, u32[]{:S(2)}) collective-permute-start(bf16[2,2,96,768]{3,2,1,0:T(8,128)(2,1)S(1)} %pad_maximum_fusion.36), channel_id=1, source_target_pairs={{0,4},{4,0},{1,5},{5,1},{2,6},{6,2},{3,7},{7,3},{8,12},{12,8},{9,1... | collective-permute-start | bytes 1769480 | tf_op jit(solution)/shard_map/ppermute | solution.py:51
  170.9 23.0 %collective-permute-start.27 = (bf16[512,768]{1,0:T(8,128)(2,1)S(1)}, bf16[512,768]{1,0:T(8,128)(2,1)S(1)}, u32[]{:S(2)}, u32[]{:S(2)}) collective-permute-start(bf16[512,768]{1,0:T(8,128)(2,1)S(1)} %fusion.37), channel_id=1, source_target_pairs={{0,1},{1,0},{2,3},{3,2},{4,5},{5,4},{6,7},{7,6},{8,9},{9,8},{10,11... | collective-permute-start | bytes 2359304 | tf_op jit(solution)/shard_map/ppermute | solution.py:51
  179.5 20.6 %collective-permute-start.53 = (bf16[2,96,768]{2,1,0:T(8,128)(2,1)S(1)}, bf16[2,96,768]{2,1,0:T(8,128)(2,1)S(1)}, u32[]{:S(2)}, u32[]{:S(2)}) collective-permute-start(bf16[2,96,768]{2,1,0:T(8,128)(2,1)S(1)} %fusion.77), channel_id=1, source_target_pairs={{0,4},{4,0},{1,5},{5,1},{2,6},{6,2},{3,7},{7,3},{8,12},{12,8},{9,1... | collective-permute-start | bytes 884744 | tf_op jit(solution)/shard_map/ppermute | solution.py:51
  181.3 17.5 %collective-permute-start.51 = (bf16[2,96,768]{2,1,0:T(8,128)(2,1)S(1)}, bf16[2,96,768]{2,1,0:T(8,128)(2,1)S(1)}, u32[]{:S(2)}, u32[]{:S(2)}) collective-permute-start(bf16[2,96,768]{2,1,0:T(8,128)(2,1)S(1)} %fusion.48), channel_id=1, source_target_pairs={{0,2},{2,0},{1,3},{3,1},{4,6},{6,4},{5,7},{7,5},{8,10},{10,8},{9,1... | collective-permute-start | bytes 884744 | tf_op jit(solution)/shard_map/ppermute | solution.py:51
  192.1 20.9 %collective-permute-start.46 = (bf16[2,96,768]{2,1,0:T(8,128)(2,1)S(1)}, bf16[2,96,768]{2,1,0:T(8,128)(2,1)S(1)}, u32[]{:S(2)}, u32[]{:S(2)}) collective-permute-start(bf16[2,96,768]{2,1,0:T(8,128)(2,1)S(1)} %fusion.76), channel_id=1, source_target_pairs={{0,4},{4,0},{1,5},{5,1},{2,6},{6,2},{3,7},{7,3},{8,12},{12,8},{9,1... | collective-permute-start | bytes 884744 | tf_op jit(solution)/shard_map/ppermute | solution.py:51
  196.7 1.3 collective-permute-start.37
  196.9 10.6 %collective-permute-start.44 = (bf16[2,96,768]{2,1,0:T(8,128)(2,1)S(1)}, bf16[2,96,768]{2,1,0:T(8,128)(2,1)S(1)}, u32[]{:S(2)}, u32[]{:S(2)}) collective-permute-start(bf16[2,96,768]{2,1,0:T(8,128)(2,1)S(1)} %fusion.52), channel_id=1, source_target_pairs={{0,2},{2,0},{1,3},{3,1},{4,6},{6,4},{5,7},{7,5},{8,10},{10,8},{9,1... | collective-permute-start | bytes 884744 | tf_op jit(solution)/shard_map/ppermute | solution.py:51
  197.6 34.7 %copy-start.45 = (bf16[512,768]{1,0:T(8,128)(2,1)}, bf16[512,768]{1,0:T(8,128)(2,1)S(1)}, u32[]{:S(2)}) copy-start(bf16[512,768]{1,0:T(8,128)(2,1)S(1)} %convert_element_type.290) | copy-start | bytes 2359300
  198.0 34.3 %collective-permute-start.28 = (bf16[512,768]{1,0:T(8,128)(2,1)S(1)}, bf16[512,768]{1,0:T(8,128)(2,1)S(1)}, u32[]{:S(2)}, u32[]{:S(2)}) collective-permute-start(bf16[512,768]{1,0:T(8,128)(2,1)S(1)} %convert_element_type.290), channel_id=1, source_target_pairs={{0,1},{1,0},{2,3},{3,2},{4,5},{5,4},{6,7},{7,6},{8,9},{9,8},{10,11... | collective-permute-start | bytes 2359304 | tf_op jit(solution)/shard_map/ppermute | solution.py:51
  200.3 13.0 %collective-permute-start.54 = (bf16[96,768]{1,0:T(8,128)(2,1)S(1)}, bf16[96,768]{1,0:T(8,128)(2,1)S(1)}, u32[]{:S(2)}, u32[]{:S(2)}) collective-permute-start(bf16[96,768]{1,0:T(8,128)(2,1)S(1)} %get-tuple-element.42), channel_id=1, source_target_pairs={{0,8},{8,16},{16,24},{24,0},{1,9},{9,17},{17,25},{25,1},{2,10},{10... | collective-permute-start | bytes 442376 | tf_op jit(solution)/shard_map/ppermute | solution.py:56
  204.2 14.4 %collective-permute-start.55 = (bf16[96,768]{1,0:T(8,128)(2,1)S(1)}, bf16[96,768]{1,0:T(8,128)(2,1)S(1)}, u32[]{:S(2)}, u32[]{:S(2)}) collective-permute-start(bf16[96,768]{1,0:T(8,128)(2,1)S(1)} %get-tuple-element.43), channel_id=1, source_target_pairs={{0,16},{8,24},{16,0},{24,8},{1,17},{9,25},{17,1},{25,9},{2,18},{10... | collective-permute-start | bytes 442376 | tf_op jit(solution)/shard_map/ppermute | solution.py:56
  207.5 21.3 %collective-permute-start.56 = (bf16[96,768]{1,0:T(8,128)(2,1)S(1)}, bf16[96,768]{1,0:T(8,128)(2,1)S(1)}, u32[]{:S(2)}, u32[]{:S(2)}) collective-permute-start(bf16[96,768]{1,0:T(8,128)(2,1)S(1)} %get-tuple-element.44), channel_id=1, source_target_pairs={{0,24},{8,0},{16,8},{24,16},{1,25},{9,1},{17,9},{25,17},{2,26},{10... | collective-permute-start | bytes 442376 | tf_op jit(solution)/shard_map/ppermute | solution.py:56
  213.2 16.4 %collective-permute-start.47 = (bf16[96,768]{1,0:T(8,128)(2,1)S(1)}, bf16[96,768]{1,0:T(8,128)(2,1)S(1)}, u32[]{:S(2)}, u32[]{:S(2)}) collective-permute-start(bf16[96,768]{1,0:T(8,128)(2,1)S(1)} %get-tuple-element.45), channel_id=1, source_target_pairs={{0,8},{8,16},{16,24},{24,0},{1,9},{9,17},{17,25},{25,1},{2,10},{10... | collective-permute-start | bytes 442376 | tf_op jit(solution)/shard_map/ppermute | solution.py:56
  213.3 16.3 %collective-permute-start.48 = (bf16[96,768]{1,0:T(8,128)(2,1)S(1)}, bf16[96,768]{1,0:T(8,128)(2,1)S(1)}, u32[]{:S(2)}, u32[]{:S(2)}) collective-permute-start(bf16[96,768]{1,0:T(8,128)(2,1)S(1)} %get-tuple-element.46), channel_id=1, source_target_pairs={{0,16},{8,24},{16,0},{24,8},{1,17},{9,25},{17,1},{25,9},{2,18},{10... | collective-permute-start | bytes 442376 | tf_op jit(solution)/shard_map/ppermute | solution.py:56
  218.6 12.8 %collective-permute-start.49 = (bf16[96,768]{1,0:T(8,128)(2,1)S(1)}, bf16[96,768]{1,0:T(8,128)(2,1)S(1)}, u32[]{:S(2)}, u32[]{:S(2)}) collective-permute-start(bf16[96,768]{1,0:T(8,128)(2,1)S(1)} %get-tuple-element.47), channel_id=1, source_target_pairs={{0,24},{8,0},{16,8},{24,16},{1,25},{9,1},{17,9},{25,17},{2,26},{10... | collective-permute-start | bytes 442376 | tf_op jit(solution)/shard_map/ppermute | solution.py:56
  312.5 16.6 %collective-permute-start.38 = (f32[6912]{0:T(1024)}, f32[6912]{0:T(1024)}, u32[]{:S(2)}, u32[]{:S(2)}) collective-permute-start(f32[6912]{0:T(1024)} %pad_maximum_fusion.39), channel_id=1, source_target_pairs={{0,4},{4,0},{1,5},{5,1},{2,6},{6,2},{3,7},{7,3},{8,12},{12,8},{9,1... | collective-permute-start | bytes 82952 | tf_op jit(solution)/shard_map/ppermute | solution.py:51
  316.6 26.7 %collective-permute-start.32 = (bf16[2,2,96,768]{3,2,0,1:T(8,128)(2,1)}, bf16[2,2,96,768]{3,2,0,1:T(8,128)(2,1)}, u32[]{:S(2)}, u32[]{:S(2)}) collective-permute-start(bf16[2,2,96,768]{3,2,0,1:T(8,128)(2,1)} %copy.68), channel_id=1, source_target_pairs={{0,2},{2,0},{1,3},{3,1},{4,6},{6,4},{5,7},{7,5},{8,10},{10,8},{9,1... | collective-permute-start | bytes 1769480 | tf_op jit(solution)/shard_map/ppermute | solution.py:51
  330.0 3.9 %collective-permute-start.39 = (f32[6912]{0:T(1024)S(1)}, f32[6912]{0:T(1024)S(1)}, u32[]{:S(2)}, u32[]{:S(2)}) collective-permute-start(f32[6912]{0:T(1024)S(1)} %fusion.186), channel_id=1, source_target_pairs={{0,2},{2,0},{1,3},{3,1},{4,6},{6,4},{5,7},{7,5},{8,10},{10,8},{9,1... | collective-permute-start | bytes 82952 | tf_op jit(solution)/shard_map/ppermute | solution.py:51
  331.2 14.6 %collective-permute-start.30 = (bf16[2,2,96,768]{3,2,1,0:T(8,128)(2,1)S(1)}, bf16[2,2,96,768]{3,2,1,0:T(8,128)(2,1)S(1)}, u32[]{:S(2)}, u32[]{:S(2)}) collective-permute-start(bf16[2,2,96,768]{3,2,1,0:T(8,128)(2,1)S(1)} %pad_maximum_fusion.35), channel_id=1, source_target_pairs={{0,4},{4,0},{1,5},{5,1},{2,6},{6,2},{3,7},{7,3},{8,12},{12,8},{9,1... | collective-permute-start | bytes 1769480 | tf_op jit(solution)/shard_map/ppermute | solution.py:51
  333.9 7.2 %collective-permute-start.40 = (f32[6912]{0:T(1024)S(1)}, f32[6912]{0:T(1024)S(1)}, u32[]{:S(2)}, u32[]{:S(2)}) collective-permute-start(f32[6912]{0:T(1024)S(1)} %add.378), channel_id=1, source_target_pairs={{0,8},{8,16},{16,24},{24,0},{1,9},{9,17},{17,25},{25,1},{2,10},{10... | collective-permute-start | bytes 82952 | tf_op jit(solution)/shard_map/ppermute | solution.py:56
  335.3 5.9 %collective-permute-start.41 = (f32[6912]{0:T(1024)S(1)}, f32[6912]{0:T(1024)S(1)}, u32[]{:S(2)}, u32[]{:S(2)}) collective-permute-start(f32[6912]{0:T(1024)S(1)} %add.378), channel_id=1, source_target_pairs={{0,16},{8,24},{16,0},{24,8},{1,17},{9,25},{17,1},{25,9},{2,18},{10... | collective-permute-start | bytes 82952 | tf_op jit(solution)/shard_map/ppermute | solution.py:56
  338.8 3.9 %collective-permute-start.42 = (f32[6912]{0:T(1024)S(1)}, f32[6912]{0:T(1024)S(1)}, u32[]{:S(2)}, u32[]{:S(2)}) collective-permute-start(f32[6912]{0:T(1024)S(1)} %add.378), channel_id=1, source_target_pairs={{0,24},{8,0},{16,8},{24,16},{1,25},{9,1},{17,9},{25,17},{2,26},{10... | collective-permute-start | bytes 82952 | tf_op jit(solution)/shard_map/ppermute | solution.py:56
  341.1 17.9 %collective-permute-start.29 = (bf16[512,768]{1,0:T(8,128)(2,1)S(1)}, bf16[512,768]{1,0:T(8,128)(2,1)S(1)}, u32[]{:S(2)}, u32[]{:S(2)}) collective-permute-start(bf16[512,768]{1,0:T(8,128)(2,1)S(1)} %add_convert_fusion), channel_id=1, source_target_pairs={{0,1},{1,0},{2,3},{3,2},{4,5},{5,4},{6,7},{7,6},{8,9},{9,8},{10,11... | collective-permute-start | bytes 2359304 | tf_op jit(solution)/shard_map/ppermute | solution.py:51
  344.6 8.0 %collective-permute-start.33 = (bf16[2,96,768]{2,1,0:T(8,128)(2,1)S(1)}, bf16[2,96,768]{2,1,0:T(8,128)(2,1)S(1)}, u32[]{:S(2)}, u32[]{:S(2)}) collective-permute-start(bf16[2,96,768]{2,1,0:T(8,128)(2,1)S(1)} %fusion.75), channel_id=1, source_target_pairs={{0,4},{4,0},{1,5},{5,1},{2,6},{6,2},{3,7},{7,3},{8,12},{12,8},{9,1... | collective-permute-start | bytes 884744 | tf_op jit(solution)/shard_map/ppermute | solution.py:51
  346.0 7.8 %collective-permute-start.31 = (bf16[2,96,768]{2,1,0:T(8,128)(2,1)S(1)}, bf16[2,96,768]{2,1,0:T(8,128)(2,1)S(1)}, u32[]{:S(2)}, u32[]{:S(2)}) collective-permute-start(bf16[2,96,768]{2,1,0:T(8,128)(2,1)S(1)} %fusion.56), channel_id=1, source_target_pairs={{0,2},{2,0},{1,3},{3,1},{4,6},{6,4},{5,7},{7,5},{8,10},{10,8},{9,1... | collective-permute-start | bytes 884744 | tf_op jit(solution)/shard_map/ppermute | solution.py:51
  354.1 8.7 %collective-permute-start.34 = (bf16[96,768]{1,0:T(8,128)(2,1)S(1)}, bf16[96,768]{1,0:T(8,128)(2,1)S(1)}, u32[]{:S(2)}, u32[]{:S(2)}) collective-permute-start(bf16[96,768]{1,0:T(8,128)(2,1)S(1)} %get-tuple-element.48), channel_id=1, source_target_pairs={{0,8},{8,16},{16,24},{24,0},{1,9},{9,17},{17,25},{25,1},{2,10},{10... | collective-permute-start | bytes 442376 | tf_op jit(solution)/shard_map/ppermute | solution.py:56
  356.2 10.6 %collective-permute-start.35 = (bf16[96,768]{1,0:T(8,128)(2,1)S(1)}, bf16[96,768]{1,0:T(8,128)(2,1)S(1)}, u32[]{:S(2)}, u32[]{:S(2)}) collective-permute-start(bf16[96,768]{1,0:T(8,128)(2,1)S(1)} %get-tuple-element.49), channel_id=1, source_target_pairs={{0,16},{8,24},{16,0},{24,8},{1,17},{9,25},{17,1},{25,9},{2,18},{10... | collective-permute-start | bytes 442376 | tf_op jit(solution)/shard_map/ppermute | solution.py:56
  359.0 7.7 %collective-permute-start.36 = (bf16[96,768]{1,0:T(8,128)(2,1)S(1)}, bf16[96,768]{1,0:T(8,128)(2,1)S(1)}, u32[]{:S(2)}, u32[]{:S(2)}) collective-permute-start(bf16[96,768]{1,0:T(8,128)(2,1)S(1)} %get-tuple-element.50), channel_id=1, source_target_pairs={{0,24},{8,0},{16,8},{24,16},{1,25},{9,1},{17,9},{25,17},{2,26},{10... | collective-permute-start | bytes 442376 | tf_op jit(solution)/shard_map/ppermute | solution.py:56
  (79 other events, 416.9 us)
